TPU v7x, 32 devices: a whole 2x2x4 slice. The times are simulated.
32 devices in a mesh: col: 2 (over x), row: 16 (over z, y, core).
Axes of the slice: x: 2, y: 2, z: 4, core: 2. Of those that a mesh axis runs over, the one named last changes fastest.
Arguments:
- residual: bfloat16 [1024, 2880], P('row'), may hold values from -6 to 6
- query_states: bfloat16 [1024, 4096], P('row', 'col'), may hold values from -48 to 48
- key_states: bfloat16 [1024, 512], P('row'), may hold values from -24 to 24
- value_states: bfloat16 [1024, 512], P('row'), may hold values from -6 to 6
- segment_ids: int32 [1024], P('row'), may hold values from 0 to 3, never falling along the last dimension, each value on 1 to 512 neighbouring positions
- sink_logits: float32 [64], P('col'), may hold values from -2 to 4
- w_out: bfloat16 [4096, 2880], P('col'), may hold values from -0.375 to 0.375
- norm_gain: float32 [2880], replicated, may hold values from 0.5 to 1.5
- expert_ids: int32 [1024, 4], P('row'), may hold values from 0 to 15, all different within a row; in each aligned block of 64 rows (0 to 63, 64 to 127, ...) at most 32 rows name the same one
- route_weight: float32 [1024, 4], P('row'), may hold values from 0.05 to 0.45
- w_gate_up: bfloat16 [16, 2, 2880, 2880], P('row', None, None, 'col'), may hold values from -0.109375 to 0.109375
- w_down: bfloat16 [16, 2880, 2880], P('row', 'col'), may hold values from -0.109375 to 0.109375
Outputs:
- layer_out: bfloat16 [1024, 2880], P('row', 'col')
Inputs may be any that keep to these rules, and one draw needn't show every extreme that they name: `expert_ids`: each token names 4 different experts; among the 64 tokens of one index of row no expert is named by more than 32 tokens, and in every draw some expert is named by exactly 32 of them. `segment_ids`: segment numbers never fall along the tokens.
All inputs are finite; a program needn't handle non-finite values.
Results may differ from a plain program's by a relative error of at most 0.018.
Values may be sent and summed in bfloat16 or wider, within the bound.
A program may use at most 128 MiB of HBM per device.

v0:
```python
import jax
import jax.numpy as jnp
from jax import lax
from jax.sharding import PartitionSpec as P

HEADS = 64
KV_HEADS = 8
HEAD_DIM = 64
WINDOW = 128
TOP = 4


epsilon = 1e-05
masked_score = -1e30


def shifted(shard, axis, by):
    size = lax.axis_size(axis)
    pairs = [(i, i + by) for i in range(size) if 0 <= i + by < size]
    return lax.ppermute(shard, axis, pairs)


def normalize(stream_rows, norm_gain):
    values32 = stream_rows.astype(jnp.float32)
    square_mean = jnp.mean(values32 * values32, axis=-1, keepdims=True)
    return (values32 * lax.rsqrt(square_mean + epsilon) * norm_gain).astype(jnp.bfloat16)


def attend(query_groups, key_groups, value_groups, allowed, sink_groups):
    scores = jnp.einsum(
        "tgjd,lgd->gjtl", query_groups, key_groups, preferred_element_type=jnp.float32
    )
    scores = scores * query_groups.shape[-1] ** (-0.5)
    scores = jnp.where(allowed[None, None], scores, masked_score)
    peak_score = jnp.maximum(jnp.max(scores, axis=-1, keepdims=True), sink_groups)
    numerator = jnp.exp(scores - peak_score)
    denominator = jnp.exp(sink_groups - peak_score) + jnp.sum(numerator, axis=-1, keepdims=True)
    weights = (numerator / denominator).astype(jnp.bfloat16)
    return jnp.einsum(
        "gjtl,lgd->tgjd", weights, value_groups, preferred_element_type=jnp.float32
    ).astype(jnp.bfloat16)


def local(
    residual,
    query_states,
    key_states,
    value_states,
    segment_ids,
    sink_logits,
    w_out,
    norm_gain,
    expert_ids,
    route_weight,
    w_gate_up,
    w_down,
):
    tok_rows = query_states.shape[0]
    row_count = lax.axis_size("row")
    col_count = lax.axis_size("col")
    row_index = lax.axis_index("row")
    col_index = lax.axis_index("col")
    local_heads = sink_logits.shape[0]
    group_size = HEADS // KV_HEADS
    if local_heads >= group_size:
        kv_count = local_heads // group_size
        kv_first = col_index * kv_count
    else:
        kv_count = 1
        kv_first = col_index * local_heads // group_size
    kv_width = kv_count * HEAD_DIM
    own_keys = lax.dynamic_slice_in_dim(key_states, kv_first * HEAD_DIM, kv_width, 1)
    own_values = lax.dynamic_slice_in_dim(value_states, kv_first * HEAD_DIM, kv_width, 1)
    shift_count = (WINDOW + tok_rows - 2) // tok_rows
    key_parts = []
    value_parts = []
    segment_parts = []
    start_parts = []
    for offset in range(shift_count, 0, -1):
        arrived = shifted((own_keys, own_values, segment_ids), "row", offset)
        key_parts.append(arrived[0])
        value_parts.append(arrived[1])
        segment_parts.append(arrived[2])
        start_parts.append((row_index - offset) * tok_rows)
    key_parts.append(own_keys)
    value_parts.append(own_values)
    segment_parts.append(segment_ids)
    start_parts.append(row_index * tok_rows)
    key_groups = jnp.concatenate(key_parts, 0).reshape(-1, kv_count, HEAD_DIM)
    value_groups = jnp.concatenate(value_parts, 0).reshape(-1, kv_count, HEAD_DIM)
    key_segments = jnp.concatenate(segment_parts, 0)
    positions = jnp.arange(tok_rows, dtype=jnp.int32)
    key_position = jnp.concatenate([start + positions for start in start_parts], 0)
    query_position = row_index * tok_rows + positions
    allowed = (key_position[None, :] >= 0) & (key_position[None, :] <= query_position[:, None])
    allowed = allowed & (key_position[None, :] > query_position[:, None] - WINDOW)
    allowed = allowed & (key_segments[None, :] == segment_ids[:, None])
    query_groups = query_states.reshape(tok_rows, kv_count, local_heads // kv_count, HEAD_DIM)
    sink_groups = sink_logits.reshape(kv_count, local_heads // kv_count, 1, 1)
    attended = attend(query_groups, key_groups, value_groups, allowed, sink_groups).reshape(
        tok_rows, local_heads * HEAD_DIM
    )
    partial_value = jnp.dot(attended, w_out, preferred_element_type=jnp.float32)
    feature_count = residual.shape[1] // col_count
    experts_all = w_gate_up.shape[0] * row_count
    slot_cap = max(2, 2 * TOP * tok_rows // experts_all)
    flat_ids = expert_ids.reshape(-1)
    expert_hot = (flat_ids[:, None] == jnp.arange(experts_all, dtype=jnp.int32)[None, :]).astype(
        jnp.int32
    )
    earlier = jnp.cumsum(expert_hot, axis=0) - expert_hot
    slot_of = jnp.sum(earlier * expert_hot, axis=1)
    slot_hot = (slot_of[:, None] == jnp.arange(slot_cap, dtype=jnp.int32)[None, :]).astype(
        jnp.float32
    )
    selector = jnp.einsum(
        "tke,tks->est",
        expert_hot.astype(jnp.float32).reshape(tok_rows, TOP, experts_all),
        slot_hot.reshape(tok_rows, TOP, slot_cap),
    )
    selector = selector.astype(jnp.bfloat16).reshape(experts_all * slot_cap, tok_rows)
    target = (flat_ids * slot_cap + slot_of).reshape(tok_rows, TOP)
    expert_gate_up = w_gate_up[0]
    expert_down = w_down[0]
    summed = lax.psum(partial_value.astype(jnp.bfloat16), "col").astype(jnp.float32)
    stream = (residual.astype(jnp.float32) + summed).astype(jnp.bfloat16)
    stream_part = lax.dynamic_slice_in_dim(stream, col_index * feature_count, feature_count, 1)
    source_rows = normalize(stream, norm_gain)
    packed = jnp.dot(selector, source_rows, preferred_element_type=jnp.float32).astype(jnp.bfloat16)
    gate_up = jnp.einsum(
        "scd,tdf->tscf",
        lax.all_to_all(
            packed.reshape(experts_all, slot_cap, source_rows.shape[1]),
            "row",
            split_axis=0,
            concat_axis=0,
            tiled=True,
        ),
        expert_gate_up,
        preferred_element_type=jnp.float32,
    )
    active = ((gate_up[1] + 1.0) * gate_up[0] * jax.nn.sigmoid(1.702 * gate_up[0])).astype(
        jnp.bfloat16
    )
    expert_partial = jnp.einsum(
        "scf,fd->scd", active, expert_down, preferred_element_type=jnp.float32
    )
    expert_result = lax.psum_scatter(
        expert_partial.astype(jnp.bfloat16), "col", scatter_dimension=2, tiled=True
    )
    returned = lax.all_to_all(expert_result, "row", split_axis=0, concat_axis=0, tiled=True)
    returned_rows = returned.reshape(experts_all * slot_cap, feature_count).astype(jnp.float32)
    picked = jnp.take(returned_rows, target, axis=0)
    expert_mix = jnp.sum(route_weight[:, :, None] * picked, axis=1)
    return (stream_part.astype(jnp.float32) + expert_mix).astype(jnp.bfloat16)


def solution(mesh):
    in_specs = (
        P("row", None),
        P("row", "col"),
        P("row", None),
        P("row", None),
        P("row"),
        P("col"),
        P("col", None),
        P(),
        P("row", None),
        P("row", None),
        P("row", None, None, "col"),
        P("row", "col", None),
    )
    out_specs = P("row", "col")
    return jax.shard_map(local, mesh=mesh, in_specs=in_specs, out_specs=out_specs, check_vma=False)
```

profile of v0, /device:TPU:0, one launch (start us, length us, event | category | flops | bytes accessed | tf_op | source)
XLA Modules:
  0.0 309.2 jit_solution(653327269411745198)
XLA Ops:
  6.5 5.0 %collective-permute-start.2 = (s32[64]{0:T(128)}, s32[64]{0:T(128)S(1)}, u32[]{:S(2)}, u32[]{:S(2)}) collective-permute-start(s32[64]{0:T(128)} %param.16), channel_id=1, source_target_pairs={{0,2},{1,3},{2,4},{3,5},{4,6},{5,7},{6,8},{7,9},{8,10},{9,11},{10,... | collective-permute-start | bytes 776 | tf_op jit(solution)/shard_map/ppermute | solution.py:20
  11.6 1.5 collective-permute-start.3
  13.1 3.9 %collective-permute-start.4 = (bf16[64,256]{1,0:T(8,128)(2,1)S(1)}, bf16[64,256]{1,0:T(8,128)(2,1)S(1)}, u32[]{:S(2)}, u32[]{:S(2)}) collective-permute-start(bf16[64,256]{1,0:T(8,128)(2,1)S(1)} %constant_dynamic-slice_fusion), channel_id=1, source_target_pairs={{0,2},{1,3},{2,4},{3,5},{4,6},{5,7},{6,8},{7,9},{8,10},{9,11},{10,... | collective-permute-start | bytes 98312 | tf_op jit(solution)/shard_map/ppermute | solution.py:20
  17.0 3.2 %collective-permute-start.5 = (bf16[64,256]{1,0:T(8,128)(2,1)S(1)}, bf16[64,256]{1,0:T(8,128)(2,1)S(1)}, u32[]{:S(2)}, u32[]{:S(2)}) collective-permute-start(bf16[64,256]{1,0:T(8,128)(2,1)S(1)} %constant_dynamic-slice_fusion), channel_id=1, source_target_pairs={{0,1},{1,2},{2,3},{3,4},{4,5},{5,6},{6,7},{7,8},{8,9},{9,10},{10,1... | collective-permute-start | bytes 98312 | tf_op jit(solution)/shard_map/ppermute | solution.py:20
  20.2 0.8 constant_dynamic-slice_fusion.1
  21.0 3.4 %collective-permute-start = (bf16[64,256]{1,0:T(8,128)(2,1)S(1)}, bf16[64,256]{1,0:T(8,128)(2,1)S(1)}, u32[]{:S(2)}, u32[]{:S(2)}) collective-permute-start(bf16[64,256]{1,0:T(8,128)(2,1)S(1)} %constant_dynamic-slice_fusion.1), channel_id=1, source_target_pairs={{0,2},{1,3},{2,4},{3,5},{4,6},{5,7},{6,8},{7,9},{8,10},{9,11},{10,... | collective-permute-start | bytes 98312 | tf_op jit(solution)/shard_map/ppermute | solution.py:20
  24.4 0.8 copy.49
  25.2 0.1 eq.70
  25.3 0.1 broadcast_compare_fusion
  25.4 1.5 reshape.222
  26.9 0.7 max.18
  27.6 0.6 reduce-window.6
  28.2 0.0 collective-permute-done.2
  28.2 1.9 collective-permute-start.1
  30.1 0.0 collective-permute-done.3
  30.1 0.7 pad_add_fusion.1
  30.9 0.7 compare_and_fusion
  31.6 0.0 collective-permute-done.4
  31.6 0.0 collective-permute-done.5
  31.7 0.1 copy.46
  31.8 0.6 fusion.36
  32.3 0.1 broadcast_maximum_fusion
  32.4 0.7 fusion.14
  33.1 0.1 exponential_add_fusion
  33.2 0.0 collective-permute-done
  33.2 0.1 copy.45
  33.3 1.1 convolution_convert_fusion.2
  34.4 0.0 copy-start.4
  34.4 8.9 %convolution_convert_fusion.1 = bf16[64,2880]{1,0:T(8,128)(2,1)} fusion(bf16[64,2048]{0,1:T(8,128)(2,1)S(1)} %bitcast.74, bf16[2048,2880]{0,1:T(8,128)(2,1)} %param.18), kind=kOutput, calls=%fused_computation.8 | convolution fusion | flops 755159040 | bytes 12427264 | tf_op jit(solution)/shard_map/dot_general | solution.py:103
  43.3 0.0 all-reduce.2.cloned.1.call-update
  43.3 0.0 reduce-scatter.4.cloned.1.call-start
  43.4 0.2 slice_reduce_fusion
  43.6 0.1 eq.66
  43.7 0.1 fusion.32
  43.8 0.1 reduce_sum.40
  43.9 0.5 fusion.18
  44.5 0.3 copy.55
  44.7 23.7 %all-reduce.2.cloned.1.call-done = bf16[64,2880]{1,0:T(8,128)(2,1)} async-done(((bf16[64,2880]{1,0:T(8,128)(2,1)}), bf16[64,2880]{1,0:T(8,128)(2,1)}) %all-reduce.2.cloned.1.call-update) | async-done | bytes 368656 | tf_op jit(solution)/shard_map/psum | solution.py:125
  68.5 1.2 fusion.19
  69.7 0.7 copy-done.2
  70.5 1.0 convolution_convert_fusion
  71.5 3.0 copy.56
  74.5 73.0 %all_to_all.10 = bf16[16,32,2880]{2,1,0:T(8,128)(2,1)S(1)} all-to-all(bf16[16,32,2880]{2,1,0:T(8,128)(2,1)} %bitcast.72), channel_id=1, replica_groups=mesh['col'=2,'row'=16] {'row'}, dimensions={0} | all-to-all | bytes 5898240 | tf_op jit(solution)/shard_map/all_to_all | solution.py:132
  147.5 15.2 %fusion.7 = f32[2,16,32,1440]{3,2,0,1:T(8,128)} fusion(bf16[1,2,2880,1440]{2,3,1,0:T(8,128)(2,1)} %param.22, bf16[16,32,2880]{2,1,0:T(8,128)(2,1)S(1)} %all_to_all.10), kind=kOutput, calls=%fused_computation.7 | convolution fusion | flops 8493465600 | bytes 25436160 | tf_op jit(solution)/shard_map/scd,tdf->tscf/dot_general | solution.py:130
  162.7 9.8 %fusion.4 = bf16[16,32,2880]{2,1,0:T(8,128)(2,1)S(1)} fusion(bf16[1,1440,2880]{2,1,0:T(8,128)(2,1)} %param.23, f32[2,16,32,1440]{3,2,0,1:T(8,128)} %fusion.7), kind=kOutput, calls=%fused_computation.5 | convolution fusion | flops 4254105600 | bytes 17141760 | tf_op jit(solution)/shard_map/scf,fd->scd/dot_general | solution.py:145
  172.5 12.1 %copy.61 = bf16[16,32,2880]{1,0,2:T(8,128)(2,1)} copy(bf16[16,32,2880]{2,1,0:T(8,128)(2,1)S(1)} %fusion.4) | data formatting | bytes 5898240
  184.6 16.3 %reshape.243 = bf16[2880,512]{1,0:T(8,128)(2,1)} reshape(bf16[2880,16,32]{2,1,0:T(8,128)(2,1)} %bitcast.70) | data formatting | bytes 5898240
  200.9 0.0 reduce-scatter.4.cloned.1.call-update
  200.9 40.5 %reduce-scatter.4.cloned.1.call-done = bf16[1440,512]{1,0:T(8,128)(2,1)} async-done(((bf16[2880,512]{1,0:T(8,128)(2,1)}), bf16[1440,512]{1,0:T(8,128)(2,1)}) %reduce-scatter.4.cloned.1.call-update) | async-done | bytes 1474576
  241.5 7.7 %reshape.244 = bf16[1440,16,32]{2,1,0:T(8,128)(2,1)} reshape(bf16[1440,512]{1,0:T(8,128)(2,1)} %reduce-scatter.4.cloned.1.call-done) | data formatting | bytes 2949120
  249.2 7.2 %copy.62 = bf16[16,32,1440]{2,1,0:T(8,128)(2,1)} copy(bf16[16,32,1440]{1,0,2:T(8,128)(2,1)} %bitcast.71) | data formatting | bytes 2949120
  256.4 5.8 %all-to-all-start.1 = ((bf16[16,32,1440]{2,1,0:T(8,128)(2,1)}), bf16[16,32,1440]{2,1,0:T(8,128)(2,1)}, u32[]{:S(2)}, u32[]{:S(2)}) async-start(bf16[16,32,1440]{2,1,0:T(8,128)(2,1)} %copy.62), calls=%async_computation.1 | async-start | bytes 3145728 | tf_op jit(solution)/shard_map/all_to_all | solution.py:151
  262.2 0.1 copy.52
  262.3 0.1 copy.57
  262.4 0.1 reshape.230
  262.5 0.1 copy.53
  262.7 0.1 copy.48
  262.8 31.4 %all-to-all-done.1 = bf16[16,32,1440]{2,1,0:T(8,128)(2,1)} async-done(((bf16[16,32,1440]{2,1,0:T(8,128)(2,1)}), bf16[16,32,1440]{2,1,0:T(8,128)(2,1)}, u32[]{:S(2)}, u32[]{:S(2)}) %all-to-all-start.1) | async-done | bytes 1474592 | tf_op jit(solution)/shard_map/all_to_all | solution.py:151
  294.1 1.8 bitcast_convert_fusion
  295.9 0.0 copy-start.1
  296.0 2.3 gather_fusion
  298.3 1.8 reshape.229
  300.1 1.4 multiply_reduce_fusion
  301.6 0.8 add_convert_fusion.1
  (26 shorter events, 0.1 us)
Async XLA Ops:
  6.5 6.5 %copy-start = (bf16[64,512]{1,0:T(8,128)(2,1)S(1)}, bf16[64,512]{1,0:T(8,128)(2,1)}, u32[]{:S(2)}) copy-start(bf16[64,512]{1,0:T(8,128)(2,1)} %param.14) | copy-start | bytes 196612
  6.5 61.9 %all-reduce.2.cloned.1.call-start = ((), (), s32[]{:S(2)}) async-start(), calls=%async_computation.3 | async-start | bytes 753664 | tf_op jit(solution)/shard_map/psum | solution.py:125
  6.5 21.7 %collective-permute-start.2 = (s32[64]{0:T(128)}, s32[64]{0:T(128)S(1)}, u32[]{:S(2)}, u32[]{:S(2)}) collective-permute-start(s32[64]{0:T(128)} %param.16), channel_id=1, source_target_pairs={{0,2},{1,3},{2,4},{3,5},{4,6},{5,7},{6,8},{7,9},{8,10},{9,11},{10,... | collective-permute-start | bytes 776 | tf_op jit(solution)/shard_map/ppermute | solution.py:20
  11.6 18.6 %collective-permute-start.3 = (s32[64]{0:T(128)}, s32[64]{0:T(128)S(1)}, u32[]{:S(2)}, u32[]{:S(2)}) collective-permute-start(s32[64]{0:T(128)} %param.16), channel_id=1, source_target_pairs={{0,1},{1,2},{2,3},{3,4},{4,5},{5,6},{6,7},{7,8},{8,9},{9,10},{10,1... | collective-permute-start | bytes 776 | tf_op jit(solution)/shard_map/ppermute | solution.py:20
  13.1 18.6 %collective-permute-start.4 = (bf16[64,256]{1,0:T(8,128)(2,1)S(1)}, bf16[64,256]{1,0:T(8,128)(2,1)S(1)}, u32[]{:S(2)}, u32[]{:S(2)}) collective-permute-start(bf16[64,256]{1,0:T(8,128)(2,1)S(1)} %constant_dynamic-slice_fusion), channel_id=1, source_target_pairs={{0,2},{1,3},{2,4},{3,5},{4,6},{5,7},{6,8},{7,9},{8,10},{9,11},{10,... | collective-permute-start | bytes 98312 | tf_op jit(solution)/shard_map/ppermute | solution.py:20
  17.0 14.7 %collective-permute-start.5 = (bf16[64,256]{1,0:T(8,128)(2,1)S(1)}, bf16[64,256]{1,0:T(8,128)(2,1)S(1)}, u32[]{:S(2)}, u32[]{:S(2)}) collective-permute-start(bf16[64,256]{1,0:T(8,128)(2,1)S(1)} %constant_dynamic-slice_fusion), channel_id=1, source_target_pairs={{0,1},{1,2},{2,3},{3,4},{4,5},{5,6},{6,7},{7,8},{8,9},{9,10},{10,1... | collective-permute-start | bytes 98312 | tf_op jit(solution)/shard_map/ppermute | solution.py:20
  21.0 12.2 %collective-permute-start = (bf16[64,256]{1,0:T(8,128)(2,1)S(1)}, bf16[64,256]{1,0:T(8,128)(2,1)S(1)}, u32[]{:S(2)}, u32[]{:S(2)}) collective-permute-start(bf16[64,256]{1,0:T(8,128)(2,1)S(1)} %constant_dynamic-slice_fusion.1), channel_id=1, source_target_pairs={{0,2},{1,3},{2,4},{3,5},{4,6},{5,7},{6,8},{7,9},{8,10},{9,11},{10,... | collective-permute-start | bytes 98312 | tf_op jit(solution)/shard_map/ppermute | solution.py:20
  28.2 5.0 %collective-permute-start.1 = (bf16[64,256]{1,0:T(8,128)(2,1)S(1)}, bf16[64,256]{1,0:T(8,128)(2,1)S(1)}, u32[]{:S(2)}, u32[]{:S(2)}) collective-permute-start(bf16[64,256]{1,0:T(8,128)(2,1)S(1)} %constant_dynamic-slice_fusion.1), channel_id=1, source_target_pairs={{0,1},{1,2},{2,3},{3,4},{4,5},{5,6},{6,7},{7,8},{8,9},{9,10},{10,1... | collective-permute-start | bytes 98312 | tf_op jit(solution)/shard_map/ppermute | solution.py:20
  34.4 34.1 %copy-start.4 = (bf16[64,2880]{1,0:T(8,128)(2,1)S(1)}, bf16[64,2880]{1,0:T(8,128)(2,1)}, u32[]{:S(2)}) copy-start(bf16[64,2880]{1,0:T(8,128)(2,1)} %param.12) | copy-start | bytes 1105924
  43.3 27.2 %copy-start.5 = (f32[2880]{0:T(1024)S(1)}, f32[2880]{0:T(1024)}, u32[]{:S(2)}) copy-start(f32[2880]{0:T(1024)} %param.19) | copy-start | bytes 34564
  43.3 198.1 %reduce-scatter.4.cloned.1.call-start = ((), (), s32[]{:S(2)}) async-start(), calls=%async_computation.4 | async-start | bytes 4423680
  69.7 0.8 copy-start.2
  256.4 5.9 %copy-start.6 = (s32[64,4]{0,1:T(4,128)S(1)}, s32[64,4]{0,1:T(4,128)}, u32[]{:S(2)}) copy-start(s32[64,4]{0,1:T(4,128)} %param.20) | copy-start | bytes 3076
  256.4 6.2 %copy-start.7 = (f32[64,4]{0,1:T(4,128)S(1)}, f32[64,4]{0,1:T(4,128)}, u32[]{:S(2)}) copy-start(f32[64,4]{0,1:T(4,128)} %param.21) | copy-start | bytes 3076
  256.4 37.7 %all-to-all-start.1 = ((bf16[16,32,1440]{2,1,0:T(8,128)(2,1)}), bf16[16,32,1440]{2,1,0:T(8,128)(2,1)}, u32[]{:S(2)}, u32[]{:S(2)}) async-start(bf16[16,32,1440]{2,1,0:T(8,128)(2,1)} %copy.62), calls=%async_computation.1 | async-start | bytes 3145728 | tf_op jit(solution)/shard_map/all_to_all | solution.py:151
  295.9 6.5 %copy-start.1 = (bf16[64,512]{1,0:T(8,128)(2,1)S(1)}, bf16[64,512]{1,0:T(8,128)(2,1)}, u32[]{:S(2)}) copy-start(bf16[64,512]{1,0:T(8,128)(2,1)} %param.14) | copy-start | bytes 196612
  298.3 3.3 %copy-start.3 = (bf16[64,2880]{1,0:T(8,128)(2,1)S(1)}, bf16[64,2880]{1,0:T(8,128)(2,1)}, u32[]{:S(2)}) copy-start(bf16[64,2880]{1,0:T(8,128)(2,1)} %copy-done.2) | copy-start | bytes 1105924
Sparse Core Ops, SparseCore 0:
  43.5 24.9 all-reduce.1
  201.1 40.3 reduce-scatter.3
where the time goes:
time: 314 us; the launch traced here: 309 us
  waiting for transfers between devices  95.7 us (30%)
  blocking collectives  73 us (23%)
  local copies, waits for them, and re-layouts  56.5 us (18%)
  matrix products  37.1 us (12%)
  starting transfers between devices  24.8 us (8%)
  between operations  13.7 us (4%)
  other arithmetic  8.42 us (3%)
    all_to_all x1, blocking collectives, local(): lax.all_to_all(packed.reshape(experts_all, slot_cap, source_rows.shape[1]...  73 us
    unnamed x22, local copies, waits for them, and re-layouts  45 us
    unnamed x3, waiting for transfers between devices  40.6 us
    all_to_all x1, waiting for transfers between devices, local(): lax.all_to_all(expert_result, 'row', split_axis=0, concat_axis=0, tiled=T...  31.4 us
    psum x1, waiting for transfers between devices, local(): lax.psum(partial_value.astype(jnp.bfloat16), 'col').astype(jnp.float32)  23.7 us
    ppermute x6, starting transfers between devices, shifted(): return lax.ppermute(shard, axis, pairs)  19 us
    dot_general x1, matrix products, local(): jnp.einsum('scd,tdf->tscf', lax.all_to_all(packed.reshape(experts_all, sl...  15.2 us
    dot_general x1, matrix products, local(): jnp.einsum('scf,fd->scd', active, expert_down, preferred_element_type=jnp...  9.79 us
  transfers between devices with their start and end apart: 9, of which 3 were waited for; matrix products, arithmetic and copies ran while one was open for 3% of the time, Pallas kernels for 0%

commit v1 on v0

--- a/solution.py
+++ b/solution.py
@@ -104,55 +104,37 @@
     feature_count = residual.shape[1] // col_count
     experts_all = w_gate_up.shape[0] * row_count
     slot_cap = max(2, 2 * TOP * tok_rows // experts_all)
-    flat_ids = expert_ids.reshape(-1)
-    expert_hot = (flat_ids[:, None] == jnp.arange(experts_all, dtype=jnp.int32)[None, :]).astype(
-        jnp.int32
-    )
-    earlier = jnp.cumsum(expert_hot, axis=0) - expert_hot
-    slot_of = jnp.sum(earlier * expert_hot, axis=1)
-    slot_hot = (slot_of[:, None] == jnp.arange(slot_cap, dtype=jnp.int32)[None, :]).astype(
-        jnp.float32
-    )
-    selector = jnp.einsum(
-        "tke,tks->est",
-        expert_hot.astype(jnp.float32).reshape(tok_rows, TOP, experts_all),
-        slot_hot.reshape(tok_rows, TOP, slot_cap),
-    )
-    selector = selector.astype(jnp.bfloat16).reshape(experts_all * slot_cap, tok_rows)
-    target = (flat_ids * slot_cap + slot_of).reshape(tok_rows, TOP)
+    routing = jnp.concatenate([expert_ids.astype(jnp.float32), route_weight], 1)
+    routing = lax.all_gather(routing, "row", axis=0, tiled=False)
+    names_mine = routing[:, :, :TOP] == row_index.astype(jnp.float32)
+    mine = jnp.any(names_mine, axis=2)
+    weight = jnp.sum(jnp.where(names_mine, routing[:, :, TOP:], 0.0), axis=2)
+    slot_of = jnp.cumsum(mine.astype(jnp.int32), axis=1) - 1
+    slots = jnp.arange(slot_cap, dtype=jnp.int32)
+    chosen = mine[:, None, :] & (slot_of[:, None, :] == slots[None, :, None])
+    selector = chosen.astype(jnp.bfloat16)
+    combine = jnp.where(chosen, weight[:, None, :], 0.0)
     expert_gate_up = w_gate_up[0]
     expert_down = w_down[0]
     summed = lax.psum(partial_value.astype(jnp.bfloat16), "col").astype(jnp.float32)
     stream = (residual.astype(jnp.float32) + summed).astype(jnp.bfloat16)
     stream_part = lax.dynamic_slice_in_dim(stream, col_index * feature_count, feature_count, 1)
     source_rows = normalize(stream, norm_gain)
-    packed = jnp.dot(selector, source_rows, preferred_element_type=jnp.float32).astype(jnp.bfloat16)
-    gate_up = jnp.einsum(
-        "scd,tdf->tscf",
-        lax.all_to_all(
-            packed.reshape(experts_all, slot_cap, source_rows.shape[1]),
-            "row",
-            split_axis=0,
-            concat_axis=0,
-            tiled=True,
-        ),
-        expert_gate_up,
-        preferred_element_type=jnp.float32,
-    )
-    active = ((gate_up[1] + 1.0) * gate_up[0] * jax.nn.sigmoid(1.702 * gate_up[0])).astype(
-        jnp.bfloat16
-    )
-    expert_partial = jnp.einsum(
-        "scf,fd->scd", active, expert_down, preferred_element_type=jnp.float32
-    )
-    expert_result = lax.psum_scatter(
-        expert_partial.astype(jnp.bfloat16), "col", scatter_dimension=2, tiled=True
-    )
-    returned = lax.all_to_all(expert_result, "row", split_axis=0, concat_axis=0, tiled=True)
-    returned_rows = returned.reshape(experts_all * slot_cap, feature_count).astype(jnp.float32)
-    picked = jnp.take(returned_rows, target, axis=0)
-    expert_mix = jnp.sum(route_weight[:, :, None] * picked, axis=1)
-    return (stream_part.astype(jnp.float32) + expert_mix).astype(jnp.bfloat16)
+    gathered = lax.all_gather(source_rows, "row", axis=0, tiled=False)
+    packed = jnp.einsum(
+        "nst,ntd->nsd", selector, gathered, preferred_element_type=jnp.float32
+    ).astype(jnp.bfloat16).reshape(row_count * slot_cap, -1)
+    gate = jnp.dot(packed, expert_gate_up[0], preferred_element_type=jnp.float32)
+    up = jnp.dot(packed, expert_gate_up[1], preferred_element_type=jnp.float32)
+    active = ((up + 1.0) * gate * jax.nn.sigmoid(1.702 * gate)).astype(jnp.bfloat16)
+    expert_partial = jnp.dot(active, expert_down, preferred_element_type=jnp.float32)
+    scaled = expert_partial.reshape(row_count, slot_cap, -1) * jnp.sum(combine, 2)[:, :, None]
+    mixed = jnp.einsum(
+        "nst,nsd->ntd", selector, scaled.astype(jnp.bfloat16), preferred_element_type=jnp.float32
+    ).astype(jnp.bfloat16).reshape(row_count * tok_rows, -1)
+    mixed = lax.psum_scatter(mixed, "row", scatter_dimension=0, tiled=True)
+    mixed = lax.psum_scatter(mixed, "col", scatter_dimension=1, tiled=True)
+    return (stream_part.astype(jnp.float32) + mixed.astype(jnp.float32)).astype(jnp.bfloat16)
 
 
 def solution(mesh):

time: 314 us -> 269 us (0.86); the launches traced: 309 us -> 269 us
  waiting for transfers between devices: 95.7 us -> 163 us
  blocking collectives: 73 us -> 22.1 us
  local copies, waits for them, and re-layouts: 56.5 us -> 9.04 us
  starting transfers between devices: 24.8 us -> 19.1 us
    reduce_scatter x0 -> x1, waiting for transfers between devices: none -> 82 us  [local(): mixed = lax.psum_scatter(mixed, 'row', scatter_dimension=0, tiled=True)]
    all_to_all x1 -> x0, blocking collectives: 73 us -> none  [local(): lax.all_to_all(packed.reshape(experts_all, slot_cap, source_rows.shape[1]...]
    unnamed x22 -> x14, local copies, waits for them, and re-layouts: 45 us -> 5.16 us
    all_gather x0 -> x1, waiting for transfers between devices: none -> 37.7 us  [local(): gathered = lax.all_gather(source_rows, 'row', axis=0, tiled=False)]
    all_to_all x1 -> x0, waiting for transfers between devices: 31.4 us -> none  [local(): lax.all_to_all(expert_result, 'row', split_axis=0, concat_axis=0, tiled=T...]
    unnamed x3 -> x5, waiting for transfers between devices: 40.6 us -> 16.4 us
    all_gather x0 -> x1, blocking collectives: none -> 22.1 us  [local(): routing = lax.all_gather(routing, 'row', axis=0, tiled=False)]
    all_to_all x1 -> x0, starting transfers between devices: 5.81 us -> none  [local(): lax.all_to_all(expert_result, 'row', split_axis=0, concat_axis=0, tiled=T...]
  transfers between devices with their start and end apart: 9 -> 10, of which waited for: 3 -> 4; matrix products, arithmetic and copies ran while one was open for 3% -> 2% of each run, Pallas kernels for 0% -> 0%
where the time goes in v1:
time: 269 us
  waiting for transfers between devices  163 us (61%)
  matrix products  36.5 us (14%)
  blocking collectives  22.1 us (8%)
  starting transfers between devices  19.1 us (7%)
  between operations  13.4 us (5%)
  local copies, waits for them, and re-layouts  9.04 us (3%)
  other arithmetic  5.84 us (2%)
    reduce_scatter x1, waiting for transfers between devices, local(): mixed = lax.psum_scatter(mixed, 'row', scatter_dimension=0, tiled=True)  82 us
    all_gather x1, waiting for transfers between devices, local(): gathered = lax.all_gather(source_rows, 'row', axis=0, tiled=False)  37.7 us
    psum x1, waiting for transfers between devices, local(): lax.psum(partial_value.astype(jnp.bfloat16), 'col').astype(jnp.float32)  26.4 us
    all_gather x1, blocking collectives, local(): routing = lax.all_gather(routing, 'row', axis=0, tiled=False)  22.1 us
    ppermute x6, starting transfers between devices, shifted(): return lax.ppermute(shard, axis, pairs)  19 us
    unnamed x5, waiting for transfers between devices  16.4 us
    dot_general x1, matrix products, local(): jnp.einsum('nst,nsd->ntd', selector, scaled.astype(jnp.bfloat16), preferr...  10.8 us
    dot_general x1, matrix products, local(): up = jnp.dot(packed, expert_gate_up[1], preferred_element_type=jnp.float32)  8.82 us
  transfers between devices with their start and end apart: 10, of which 4 were waited for; matrix products, arithmetic and copies ran while one was open for 2% of the time, Pallas kernels for 0%

profile of v1, /device:TPU:0, one launch (start us, length us, event | category | flops | bytes accessed | tf_op | source)
XLA Modules:
  0.0 268.6 jit_solution(8531859856784551742)
XLA Ops:
  6.5 0.0 copy-start
  6.5 0.0 all-reduce.2.cloned.1.call-start
  6.5 2.5 collective-permute-start.3
  9.1 4.4 %collective-permute-start.2 = (s32[64]{0:T(128)}, s32[64]{0:T(128)S(1)}, u32[]{:S(2)}, u32[]{:S(2)}) collective-permute-start(s32[64]{0:T(128)} %param.16), channel_id=1, source_target_pairs={{0,2},{1,3},{2,4},{3,5},{4,6},{5,7},{6,8},{7,9},{8,10},{9,11},{10,... | collective-permute-start | bytes 776 | tf_op jit(solution)/shard_map/ppermute | solution.py:20
  13.5 0.0 copy-done
  13.5 3.2 %collective-permute-start.1 = (bf16[64,256]{1,0:T(8,128)(2,1)S(1)}, bf16[64,256]{1,0:T(8,128)(2,1)S(1)}, u32[]{:S(2)}, u32[]{:S(2)}) collective-permute-start(bf16[64,256]{1,0:T(8,128)(2,1)S(1)} %constant_dynamic-slice_fusion.1), channel_id=1, source_target_pairs={{0,1},{1,2},{2,3},{3,4},{4,5},{5,6},{6,7},{7,8},{8,9},{9,10},{10,1... | collective-permute-start | bytes 98312 | tf_op jit(solution)/shard_map/ppermute | solution.py:20
  16.8 3.4 %collective-permute-start = (bf16[64,256]{1,0:T(8,128)(2,1)S(1)}, bf16[64,256]{1,0:T(8,128)(2,1)S(1)}, u32[]{:S(2)}, u32[]{:S(2)}) collective-permute-start(bf16[64,256]{1,0:T(8,128)(2,1)S(1)} %constant_dynamic-slice_fusion.1), channel_id=1, source_target_pairs={{0,2},{1,3},{2,4},{3,5},{4,6},{5,7},{6,8},{7,9},{8,10},{9,11},{10,... | collective-permute-start | bytes 98312 | tf_op jit(solution)/shard_map/ppermute | solution.py:20
  20.2 0.8 constant_dynamic-slice_fusion
  21.0 1.9 collective-permute-start.5
  22.9 0.1 broadcast_compare_fusion
  23.0 0.7 max.18
  23.8 1.5 reshape.191
  25.2 0.0 collective-permute-done.3
  25.2 3.4 %collective-permute-start.4 = (bf16[64,256]{1,0:T(8,128)(2,1)S(1)}, bf16[64,256]{1,0:T(8,128)(2,1)S(1)}, u32[]{:S(2)}, u32[]{:S(2)}) collective-permute-start(bf16[64,256]{1,0:T(8,128)(2,1)S(1)} %constant_dynamic-slice_fusion), channel_id=1, source_target_pairs={{0,2},{1,3},{2,4},{3,5},{4,6},{5,7},{6,8},{7,9},{8,10},{9,11},{10,... | collective-permute-start | bytes 98312 | tf_op jit(solution)/shard_map/ppermute | solution.py:20
  28.7 0.0 collective-permute-done.2
  28.7 0.7 pad_add_fusion.1
  29.4 0.7 compare_and_fusion
  30.2 0.0 collective-permute-done.1
  30.2 0.0 collective-permute-done
  30.2 0.1 copy.20
  30.3 0.0 collective-permute-done.5
  30.3 0.0 collective-permute-done.4
  30.4 0.1 copy.21
  30.5 0.0 copy-start.1
  30.5 0.6 fusion.37
  31.0 0.1 broadcast_maximum_fusion
  31.1 0.7 fusion.22
  31.8 0.1 exponential_add_fusion
  31.9 1.1 convolution_convert_fusion.3
  33.0 1.9 copy-done.1
  34.8 0.0 copy-start.2
  34.8 0.0 copy-start.3
  34.8 0.0 copy-start.4
  34.8 0.0 copy-start.5
  34.8 4.4 %convolution_convert_fusion.2 = bf16[64,2880]{1,0:T(8,128)(2,1)} fusion(bf16[64,2048]{0,1:T(8,128)(2,1)S(1)} %bitcast.59, bf16[2048,2880]{0,1:T(8,128)(2,1)S(1)} %copy-done.1), kind=kOutput, calls=%fused_computation.11 | convolution fusion | flops 755159040 | bytes 12427264 | tf_op jit(solution)/shard_map/dot_general | solution.py:103
  39.3 0.0 all-reduce.2.cloned.1.call-update
  39.3 0.0 all-gather.5.cloned.1.call-start
  39.3 26.4 %all-reduce.2.cloned.1.call-done = bf16[64,2880]{1,0:T(8,128)(2,1)} async-done(((bf16[64,2880]{1,0:T(8,128)(2,1)}), bf16[64,2880]{1,0:T(8,128)(2,1)}) %all-reduce.2.cloned.1.call-update) | async-done | bytes 368656 | tf_op jit(solution)/shard_map/psum | solution.py:119
  65.7 0.0 copy-done.2
  65.7 1.2 fusion.23
  67.0 0.0 copy-done.3
  67.0 0.9 fusion.25
  67.9 0.0 all-gather.5.cloned.1.call-update
  67.9 0.0 reduce-scatter.5.cloned.1.call-start
  68.0 0.0 copy-done.4
  68.0 0.0 copy-done.5
  68.0 22.1 %all-gather.2 = f32[16,64,8]{1,2,0:T(8,128)S(1)} all-gather(f32[1,64,8]{1,2,0:T(8,128)S(1)} %maximum_bitcast_fusion), channel_id=2, replica_groups=mesh['col'=2,'row'=16] {'row'}, dimensions={0}, use_global_device_ids=true | all-gather | bytes 34816 | tf_op jit(solution)/shard_map/all_gather | solution.py:108
  90.2 0.2 reduce_window_sum.11
  90.5 0.1 select_reduce_fusion
  90.6 37.7 %all-gather.5.cloned.1.call-done = bf16[1024,2880]{1,0:T(8,128)(2,1)} async-done(((bf16[64,2880]{1,0:T(8,128)(2,1)}), bf16[1024,2880]{1,0:T(8,128)(2,1)}) %all-gather.5.cloned.1.call-update) | async-done | bytes 5898256 | tf_op jit(solution)/shard_map/all_gather | solution.py:123
  128.4 3.7 %convolution_convert_fusion.1 = bf16[16,32,2880]{2,1,0:T(8,128)(2,1)S(1)} fusion(bf16[16,64,2880]{2,1,0:T(8,128)(2,1)} %bitcast.54, s32[16,64]{1,0:T(8,128)S(1)} %broadcast_add_fusion, pred[16,64]{1,0:T(8,128)(4,1)S(1)} %reduce_or.9), kind=kOutput, calls=%fused_computation.10 | convolution fusion | flops 190283776 | bytes 8852480 | tf_op jit(solution)/shard_map/nst,ntd->nsd/dot_general | solution.py:124
  132.0 7.2 %fusion.2 = f32[512,1440]{0,1:T(8,128)S(1)} fusion(bf16[512,2880]{1,0:T(8,128)(2,1)S(1)} %bitcast.55, bf16[1,2,2880,1440]{2,3,1,0:T(8,128)(2,1)} %param.22), kind=kOutput, calls=%fused_computation.2 | convolution fusion | flops 4246732800 | bytes 14376960 | tf_op jit(solution)/shard_map/dot_general | solution.py:127
  139.2 8.8 %fusion.19 = bf16[512,1440]{0,1:T(8,128)(2,1)S(1)} fusion(f32[512,1440]{0,1:T(8,128)S(1)} %fusion.2, bf16[512,2880]{1,0:T(8,128)(2,1)S(1)} %bitcast.56, bf16[1,2,2880,1440]{2,3,1,0:T(8,128)(2,1)} %param.22), kind=kOutput, calls=%fused_computation.15 | convolution fusion | flops 4252631040 | bytes 15851520 | tf_op jit(solution)/shard_map/dot_general | solution.py:128
  148.1 0.7 copy.23
  148.8 10.8 %convolution_convert_fusion = bf16[16,64,2880]{2,1,0:T(8,128)(2,1)} fusion(bf16[16,32,1440]{2,1,0:T(8,128)(2,1)S(1)} %bitcast.58, bf16[1,1440,2880]{2,1,0:T(8,128)(2,1)} %param.23, f32[16,32]{1,0:T(8,128)S(1)} %select_reduce_fusion, s32[16,64]{1,0:T(8,128)S(1)} %broadcast_add_fusion, pred[16,64]{1,0:T(8,128)(4,1)S(1)} %reduce_or.9), kind=kOutput, calls=%fused_computation.9 | convolution fusion | flops 4441440256 | bytes 15674368 | tf_op jit(solution)/shard_map/nst,nsd->ntd/dot_general | solution.py:132
  159.6 0.0 reduce-scatter.5.cloned.1.call-update
  159.6 0.0 reduce-scatter.7.cloned.1.call-start
  159.6 82.0 %reduce-scatter.5.cloned.1.call-done = bf16[64,2880]{1,0:T(8,128)(2,1)} async-done(((bf16[1024,2880]{1,0:T(8,128)(2,1)}), bf16[64,2880]{1,0:T(8,128)(2,1)}) %reduce-scatter.5.cloned.1.call-update) | async-done | bytes 368656 | tf_op jit(solution)/shard_map/reduce_scatter | solution.py:135
  241.6 2.1 copy.26
  243.7 0.0 reduce-scatter.7.cloned.1.call-update
  243.8 16.3 %reduce-scatter.7.cloned.1.call-done = bf16[1440,64]{1,0:T(8,128)(2,1)} async-done(((bf16[2880,64]{1,0:T(8,128)(2,1)}), bf16[1440,64]{1,0:T(8,128)(2,1)}) %reduce-scatter.7.cloned.1.call-update) | async-done | bytes 184336
  260.1 1.1 copy.27
  261.2 0.8 add_convert_fusion.1
  (12 shorter events, 0.1 us)
Async XLA Ops:
  6.5 7.0 %copy-start = (bf16[64,512]{1,0:T(8,128)(2,1)S(1)}, bf16[64,512]{1,0:T(8,128)(2,1)}, u32[]{:S(2)}) copy-start(bf16[64,512]{1,0:T(8,128)(2,1)} %param.15) | copy-start | bytes 196612
  6.5 59.2 %all-reduce.2.cloned.1.call-start = ((), (), s32[]{:S(2)}) async-start(), calls=%async_computation.2 | async-start | bytes 753664 | tf_op jit(solution)/shard_map/psum | solution.py:119
  6.5 18.7 %collective-permute-start.3 = (s32[64]{0:T(128)}, s32[64]{0:T(128)S(1)}, u32[]{:S(2)}, u32[]{:S(2)}) collective-permute-start(s32[64]{0:T(128)} %param.16), channel_id=1, source_target_pairs={{0,1},{1,2},{2,3},{3,4},{4,5},{5,6},{6,7},{7,8},{8,9},{9,10},{10,1... | collective-permute-start | bytes 776 | tf_op jit(solution)/shard_map/ppermute | solution.py:20
  9.1 19.6 %collective-permute-start.2 = (s32[64]{0:T(128)}, s32[64]{0:T(128)S(1)}, u32[]{:S(2)}, u32[]{:S(2)}) collective-permute-start(s32[64]{0:T(128)} %param.16), channel_id=1, source_target_pairs={{0,2},{1,3},{2,4},{3,5},{4,6},{5,7},{6,8},{7,9},{8,10},{9,11},{10,... | collective-permute-start | bytes 776 | tf_op jit(solution)/shard_map/ppermute | solution.py:20
  13.5 16.6 %collective-permute-start.1 = (bf16[64,256]{1,0:T(8,128)(2,1)S(1)}, bf16[64,256]{1,0:T(8,128)(2,1)S(1)}, u32[]{:S(2)}, u32[]{:S(2)}) collective-permute-start(bf16[64,256]{1,0:T(8,128)(2,1)S(1)} %constant_dynamic-slice_fusion.1), channel_id=1, source_target_pairs={{0,1},{1,2},{2,3},{3,4},{4,5},{5,6},{6,7},{7,8},{8,9},{9,10},{10,1... | collective-permute-start | bytes 98312 | tf_op jit(solution)/shard_map/ppermute | solution.py:20
  16.8 13.4 %collective-permute-start = (bf16[64,256]{1,0:T(8,128)(2,1)S(1)}, bf16[64,256]{1,0:T(8,128)(2,1)S(1)}, u32[]{:S(2)}, u32[]{:S(2)}) collective-permute-start(bf16[64,256]{1,0:T(8,128)(2,1)S(1)} %constant_dynamic-slice_fusion.1), channel_id=1, source_target_pairs={{0,2},{1,3},{2,4},{3,5},{4,6},{5,7},{6,8},{7,9},{8,10},{9,11},{10,... | collective-permute-start | bytes 98312 | tf_op jit(solution)/shard_map/ppermute | solution.py:20
  21.0 9.3 %collective-permute-start.5 = (bf16[64,256]{1,0:T(8,128)(2,1)S(1)}, bf16[64,256]{1,0:T(8,128)(2,1)S(1)}, u32[]{:S(2)}, u32[]{:S(2)}) collective-permute-start(bf16[64,256]{1,0:T(8,128)(2,1)S(1)} %constant_dynamic-slice_fusion), channel_id=1, source_target_pairs={{0,1},{1,2},{2,3},{3,4},{4,5},{5,6},{6,7},{7,8},{8,9},{9,10},{10,1... | collective-permute-start | bytes 98312 | tf_op jit(solution)/shard_map/ppermute | solution.py:20
  25.2 5.1 %collective-permute-start.4 = (bf16[64,256]{1,0:T(8,128)(2,1)S(1)}, bf16[64,256]{1,0:T(8,128)(2,1)S(1)}, u32[]{:S(2)}, u32[]{:S(2)}) collective-permute-start(bf16[64,256]{1,0:T(8,128)(2,1)S(1)} %constant_dynamic-slice_fusion), channel_id=1, source_target_pairs={{0,2},{1,3},{2,4},{3,5},{4,6},{5,7},{6,8},{7,9},{8,10},{9,11},{10,... | collective-permute-start | bytes 98312 | tf_op jit(solution)/shard_map/ppermute | solution.py:20
  30.5 4.4 %copy-start.1 = (bf16[2048,2880]{0,1:T(8,128)(2,1)S(1)}, bf16[2048,2880]{0,1:T(8,128)(2,1)}, u32[]{:S(2)}) copy-start(bf16[2048,2880]{0,1:T(8,128)(2,1)} %param.18) | copy-start | bytes 35389444
  34.8 30.9 %copy-start.2 = (bf16[64,2880]{1,0:T(8,128)(2,1)S(1)}, bf16[64,2880]{1,0:T(8,128)(2,1)}, u32[]{:S(2)}) copy-start(bf16[64,2880]{1,0:T(8,128)(2,1)} %param.12) | copy-start | bytes 1105924
  34.8 32.2 %copy-start.3 = (f32[2880]{0:T(1024)S(1)}, f32[2880]{0:T(1024)}, u32[]{:S(2)}) copy-start(f32[2880]{0:T(1024)} %param.19) | copy-start | bytes 34564
  34.8 33.2 %copy-start.4 = (s32[64,4]{0,1:T(4,128)S(1)}, s32[64,4]{0,1:T(4,128)}, u32[]{:S(2)}) copy-start(s32[64,4]{0,1:T(4,128)} %param.20) | copy-start | bytes 3076
  34.8 33.2 %copy-start.5 = (f32[64,4]{0,1:T(4,128)S(1)}, f32[64,4]{0,1:T(4,128)}, u32[]{:S(2)}) copy-start(f32[64,4]{0,1:T(4,128)} %param.21) | copy-start | bytes 3076
  39.3 89.1 %all-gather.5.cloned.1.call-start = ((), (), s32[]{:S(2)}) async-start(), calls=%async_computation.4 | async-start | bytes 6406144 | tf_op jit(solution)/shard_map/all_gather | solution.py:123
  67.9 173.7 %reduce-scatter.5.cloned.1.call-start = ((), (), s32[]{:S(2)}) async-start(), calls=%async_computation.3 | async-start | bytes 6406144 | tf_op jit(solution)/shard_map/reduce_scatter | solution.py:135
  159.6 100.5 %reduce-scatter.7.cloned.1.call-start = ((), (), s32[]{:S(2)}) async-start(), calls=%async_computation.5 | async-start | bytes 1105920
Sparse Core Ops, SparseCore 0:
  39.4 26.2 all-reduce.1
  68.0 60.2 all-gather.4
  159.7 81.8 reduce-scatter.4
  243.9 16.1 reduce-scatter.6

commit v2 on v1

--- a/solution.py
+++ b/solution.py
@@ -1,6 +1,8 @@
 import jax
 import jax.numpy as jnp
 from jax import lax
+from jax.experimental import pallas as pl
+from jax.experimental.pallas import tpu as pltpu
 from jax.sharding import PartitionSpec as P
 
 HEADS = 64
@@ -39,6 +41,302 @@
     return jnp.einsum(
         "gjtl,lgd->tgjd", weights, value_groups, preferred_element_type=jnp.float32
     ).astype(jnp.bfloat16)
+
+
+MESH = pl.DeviceIdType.MESH
+VMEM = pl.BlockSpec(memory_space=pltpu.VMEM)
+HALVES = 2
+VMEM_BYTES = 60 * 1024 * 1024
+
+
+def ring_place(row, chips):
+    chip = lax.div(row, 2)
+    along = lax.div(chip, 2)
+    return jnp.where(lax.rem(chip, 2) == 0, along, chips - 1 - along)
+
+
+def ring_row(place, chips, core):
+    place = lax.rem(place + chips, chips)
+    chip = jnp.where(place < chips // 2, 2 * place, 2 * (chips - 1 - place) + 1)
+    return 2 * chip + core
+
+
+def greet(devices):
+    barrier = pltpu.get_barrier_semaphore()
+    for device in devices:
+        pl.semaphore_signal(barrier, inc=1, device_id=device, device_id_type=MESH)
+    pl.semaphore_wait(barrier, len(devices))
+
+
+def remote(src, dst, send, recv, device):
+    return pltpu.make_async_remote_copy(
+        src_ref=src, dst_ref=dst, send_sem=send, recv_sem=recv, device_id=device,
+        device_id_type=MESH,
+    )
+
+
+def halo_kernel(rows, shifts, kv_ref, meta_ref, kv_out, meta_out, kv_send, kv_recv, m_send, m_recv, l_sem):
+    row = lax.axis_index("row")
+    others = [{"row": lax.rem(row + step, rows)} for step in range(1, rows)]
+    greet(others)
+    copies = []
+    for shift in range(1, shifts + 1):
+        copies.append(
+            remote(kv_ref, kv_out.at[shift - 1], kv_send.at[shift - 1], kv_recv.at[shift - 1],
+                   others[shift - 1])
+        )
+    for step in range(1, rows):
+        copies.append(
+            remote(meta_ref, meta_out.at[row], m_send.at[step - 1], m_recv.at[step - 1],
+                   others[step - 1])
+        )
+    for copy in copies:
+        copy.start()
+    mine = pltpu.make_async_copy(meta_ref, meta_out.at[row], l_sem)
+    mine.start()
+    for shift in range(1, shifts + 1):
+        copies[shift - 1].wait()
+    for step in range(1, rows):
+        copies[shifts + step - 1].wait_send()
+        source = lax.rem(row - step + rows, rows)
+        remote(meta_ref, meta_out.at[source], m_send.at[step - 1], m_recv.at[step - 1],
+               others[step - 1]).wait_recv()
+    mine.wait()
+
+
+def halo(kv, meta, rows, shifts):
+    return pl.pallas_call(
+        lambda *refs: halo_kernel(rows, shifts, *refs),
+        out_shape=(
+            jax.ShapeDtypeStruct((shifts, *kv.shape), kv.dtype),
+            jax.ShapeDtypeStruct((rows, *meta.shape), meta.dtype),
+        ),
+        in_specs=[VMEM] * 2,
+        out_specs=(VMEM, VMEM),
+        scratch_shapes=[
+            pltpu.SemaphoreType.DMA((shifts,)),
+            pltpu.SemaphoreType.DMA((shifts,)),
+            pltpu.SemaphoreType.DMA((rows,)),
+            pltpu.SemaphoreType.DMA((rows,)),
+            pltpu.SemaphoreType.DMA,
+        ],
+        compiler_params=pltpu.CompilerParams(
+            collective_id=1, has_side_effects=True, vmem_limit_bytes=16 * 1024 * 1024
+        ),
+        name="halo",
+    )(kv, meta)
+
+
+def ring_halves(distance, half_way, way):
+    return range(HALVES) if distance < half_way else [way]
+
+
+def spread_kernel(rows, partial_ref, residual_ref, gain_ref, stream_ref, out_ref, part_in,
+                  x_sem, send, recv, sib_send, sib_recv):
+    chips = rows // 2
+    half_way = chips // 2
+    row = lax.axis_index("row")
+    col = lax.axis_index("col")
+    core = lax.rem(row, 2)
+    place = ring_place(row, chips)
+    sibling = {"row": row + 1 - 2 * core}
+    partner = {"col": 1 - col}
+    ways = [{"row": ring_row(place + 1, chips, core)}, {"row": ring_row(place - 1, chips, core)}]
+    greet([sibling, partner] + ways)
+    cross = remote(partial_ref, part_in, x_sem.at[0], x_sem.at[1], partner)
+    cross.start()
+    cross.wait()
+    size = partial_ref.shape[0] // HALVES
+    for half in range(HALVES):
+        at = pl.ds(half * size, size)
+        summed = partial_ref[at, :].astype(jnp.float32) + part_in[at, :].astype(jnp.float32)
+        stream = (residual_ref[at, :].astype(jnp.float32) + summed).astype(jnp.bfloat16)
+        stream_ref[at, :] = stream
+        out_ref[row, at, :] = normalize(stream, gain_ref[...])
+
+    def piece(source, half, which):
+        return out_ref.at[ring_row(place + source, chips, which), pl.ds(half * size, size)]
+
+    def hop(way, distance, half):
+        source = -distance if way == 0 else distance
+        back = source + (1 if way == 0 else -1)
+        return remote(piece(back, half, core), piece(back, half, core),
+                      send.at[way, distance - 1, half], recv.at[way, distance - 1, half], ways[way])
+
+    def landed(way, distance, half):
+        source = -distance if way == 0 else distance
+        return remote(piece(source, half, core), piece(source, half, core),
+                      send.at[way, distance - 1, half], recv.at[way, distance - 1, half], ways[way])
+
+    def pass_on(way, distance, half, which):
+        source = -distance if way == 0 else distance
+        return remote(piece(source, half, which), piece(source, half, which),
+                      sib_send.at[way, distance, half], sib_recv.at[way, distance, half], sibling)
+
+    sent = []
+    for half in range(HALVES):
+        for way in range(2):
+            if half in ring_halves(1, half_way, way):
+                copy = hop(way, 1, half)
+                copy.start()
+                sent.append(copy)
+        copy = pass_on(0, 0, half, core)
+        copy.start()
+        sent.append(copy)
+    for distance in range(1, half_way + 1):
+        for half in range(HALVES):
+            for way in range(2):
+                if half not in ring_halves(distance, half_way, way):
+                    continue
+                landed(way, distance, half).wait_recv()
+                if distance < half_way and half in ring_halves(distance + 1, half_way, way):
+                    copy = hop(way, distance + 1, half)
+                    copy.start()
+                    sent.append(copy)
+                copy = pass_on(way, distance, half, core)
+                copy.start()
+                sent.append(copy)
+    for half in range(HALVES):
+        pass_on(0, 0, half, 1 - core).wait_recv()
+    for distance in range(1, half_way + 1):
+        for half in range(HALVES):
+            for way in range(2):
+                if half in ring_halves(distance, half_way, way):
+                    pass_on(way, distance, half, 1 - core).wait_recv()
+    for copy in sent:
+        copy.wait_send()
+
+
+def spread(partial, residual, gain, rows):
+    half_way = rows // 4
+    return pl.pallas_call(
+        lambda *refs: spread_kernel(rows, *refs),
+        out_shape=(
+            jax.ShapeDtypeStruct(residual.shape, jnp.bfloat16),
+            jax.ShapeDtypeStruct((rows, *residual.shape), jnp.bfloat16),
+        ),
+        in_specs=[VMEM] * 3,
+        out_specs=(VMEM, VMEM),
+        scratch_shapes=[
+            pltpu.VMEM(residual.shape, jnp.bfloat16),
+            pltpu.SemaphoreType.DMA((2,)),
+            pltpu.SemaphoreType.DMA((2, half_way, HALVES)),
+            pltpu.SemaphoreType.DMA((2, half_way, HALVES)),
+            pltpu.SemaphoreType.DMA((2, half_way + 1, HALVES)),
+            pltpu.SemaphoreType.DMA((2, half_way + 1, HALVES)),
+        ],
+        compiler_params=pltpu.CompilerParams(
+            collective_id=2, has_side_effects=True, vmem_limit_bytes=VMEM_BYTES
+        ),
+        name="spread",
+    )(partial, residual, gain.reshape(1, -1))
+
+
+def fold_kernel(rows, part_ref, out_ref, sib_buf, ring_in, ring_out, x_out, x_in,
+                x_sem, send, recv, sib_send, sib_recv):
+    chips = rows // 2
+    half_way = chips // 2
+    row = lax.axis_index("row")
+    col = lax.axis_index("col")
+    core = lax.rem(row, 2)
+    place = ring_place(row, chips)
+    sibling = {"row": row + 1 - 2 * core}
+    partner = {"col": 1 - col}
+    ways = [{"row": ring_row(place + 1, chips, core)}, {"row": ring_row(place - 1, chips, core)}]
+    greet([sibling, partner] + ways)
+    order = [half_way]
+    for distance in range(half_way - 1, 0, -1):
+        order += [distance, chips - distance]
+    order.append(0)
+    shared = {}
+    for offset in order:
+        copy = remote(part_ref.at[ring_row(place + offset, chips, 1 - core)], sib_buf.at[offset],
+                      sib_send.at[offset], sib_recv.at[offset], sibling)
+        copy.start()
+        shared[offset] = copy
+    size = part_ref.shape[1] // HALVES
+    seen = set()
+
+    def own(offset, half):
+        if offset not in seen:
+            shared[offset].wait_recv()
+            seen.add(offset)
+        at = pl.ds(half * size, size)
+        return part_ref[ring_row(place + offset, chips, core), at, :].astype(
+            jnp.float32
+        ) + sib_buf[offset, at, :].astype(jnp.float32)
+
+    def hop(way, distance, half):
+        at = pl.ds(half * size, size)
+        return remote(ring_out.at[way, distance - 1, at], ring_in.at[way, distance - 1, at],
+                      send.at[way, distance - 1, half], recv.at[way, distance - 1, half], ways[way])
+
+    def arrived(way, distance, half):
+        hop(way, distance, half).wait_recv()
+        return ring_in[way, distance - 1, pl.ds(half * size, size), :].astype(jnp.float32)
+
+    sent = []
+    for distance in range(half_way, 0, -1):
+        for half in range(HALVES):
+            for way in range(2):
+                if half not in ring_halves(distance, half_way, way):
+                    continue
+                value = own(distance if way == 0 else chips - distance, half)
+                if distance < half_way and half in ring_halves(distance + 1, half_way, way):
+                    value = value + arrived(way, distance + 1, half)
+                ring_out[way, distance - 1, pl.ds(half * size, size), :] = value.astype(jnp.bfloat16)
+                copy = hop(way, distance, half)
+                copy.start()
+                sent.append(copy)
+    width = out_ref.shape[1]
+    crosses = []
+    for half in range(HALVES):
+        at = pl.ds(half * size, size)
+        value = own(0, half)
+        for way in range(2):
+            if half in ring_halves(1, half_way, way):
+                value = value + arrived(way, 1, half)
+        low, high = value[:, :width], value[:, width:]
+        x_out[at, :] = jnp.where(col == 0, high, low).astype(jnp.bfloat16)
+        out_ref[at, :] = jnp.where(col == 0, low, high)
+        copy = remote(x_out.at[at], x_in.at[at], x_sem.at[0, half], x_sem.at[1, half], partner)
+        copy.start()
+        crosses.append(copy)
+    for half in range(HALVES):
+        at = pl.ds(half * size, size)
+        crosses[half].wait()
+        out_ref[at, :] += x_in[at, :].astype(jnp.float32)
+    for copy in sent:
+        copy.wait_send()
+    for offset in order:
+        shared[offset].wait_send()
+
+
+def fold(part, rows, width):
+    half_way = rows // 4
+    block = part.shape[1:]
+    return pl.pallas_call(
+        lambda *refs: fold_kernel(rows, *refs),
+        out_shape=jax.ShapeDtypeStruct((block[0], width), jnp.float32),
+        in_specs=[VMEM],
+        out_specs=VMEM,
+        scratch_shapes=[
+            pltpu.VMEM((rows // 2, *block), jnp.bfloat16),
+            pltpu.VMEM((2, half_way, *block), jnp.bfloat16),
+            pltpu.VMEM((2, half_way, *block), jnp.bfloat16),
+            pltpu.VMEM((block[0], width), jnp.bfloat16),
+            pltpu.VMEM((block[0], width), jnp.bfloat16),
+            pltpu.SemaphoreType.DMA((2, HALVES)),
+            pltpu.SemaphoreType.DMA((2, half_way, HALVES)),
+            pltpu.SemaphoreType.DMA((2, half_way, HALVES)),
+            pltpu.SemaphoreType.DMA((rows // 2,)),
+            pltpu.SemaphoreType.DMA((rows // 2,)),
+        ],
+        compiler_params=pltpu.CompilerParams(
+            collective_id=3, has_side_effects=True, vmem_limit_bytes=VMEM_BYTES
+        ),
+        name="fold",
+    )(part)
 
 
 def local(
@@ -72,12 +370,36 @@
     own_keys = lax.dynamic_slice_in_dim(key_states, kv_first * HEAD_DIM, kv_width, 1)
     own_values = lax.dynamic_slice_in_dim(value_states, kv_first * HEAD_DIM, kv_width, 1)
     shift_count = (WINDOW + tok_rows - 2) // tok_rows
+    block_bytes = 2 * residual.shape[0] * residual.shape[1]
+    in_kernels = (
+        col_count == 2 and row_count % 4 == 0 and row_count >= 8
+        and 4 * row_count * block_bytes < VMEM_BYTES
+    )
+    routing = jnp.concatenate([expert_ids.astype(jnp.float32), route_weight], 1).T
     key_parts = []
     value_parts = []
     segment_parts = []
     start_parts = []
+    if in_kernels:
+        own_pair = jnp.concatenate([own_keys, own_values], 1)
+        meta = jnp.concatenate(
+            [routing, jnp.broadcast_to(segment_ids.astype(jnp.float32)[None], (8, tok_rows))], 0
+        )
+        pairs, metas = halo(own_pair, meta, row_count, shift_count)
+        routing = metas[:, : 2 * TOP]
+        all_segments = metas[:, 2 * TOP].astype(jnp.int32)
+    else:
+        routing = lax.all_gather(routing, "row", axis=0, tiled=False)
     for offset in range(shift_count, 0, -1):
-        arrived = shifted((own_keys, own_values, segment_ids), "row", offset)
+        if in_kernels:
+            before = lax.rem(row_index - offset + row_count, row_count)
+            arrived = (
+                pairs[offset - 1][:, :kv_width],
+                pairs[offset - 1][:, kv_width:],
+                lax.dynamic_index_in_dim(all_segments, before, 0, keepdims=False),
+            )
+        else:
+            arrived = shifted((own_keys, own_values, segment_ids), "row", offset)
         key_parts.append(arrived[0])
         value_parts.append(arrived[1])
         segment_parts.append(arrived[2])
@@ -104,11 +426,9 @@
     feature_count = residual.shape[1] // col_count
     experts_all = w_gate_up.shape[0] * row_count
     slot_cap = max(2, 2 * TOP * tok_rows // experts_all)
-    routing = jnp.concatenate([expert_ids.astype(jnp.float32), route_weight], 1)
-    routing = lax.all_gather(routing, "row", axis=0, tiled=False)
-    names_mine = routing[:, :, :TOP] == row_index.astype(jnp.float32)
-    mine = jnp.any(names_mine, axis=2)
-    weight = jnp.sum(jnp.where(names_mine, routing[:, :, TOP:], 0.0), axis=2)
+    names_mine = routing[:, :TOP] == row_index.astype(jnp.float32)
+    mine = jnp.any(names_mine, axis=1)
+    weight = jnp.sum(jnp.where(names_mine, routing[:, TOP:], 0.0), axis=1)
     slot_of = jnp.cumsum(mine.astype(jnp.int32), axis=1) - 1
     slots = jnp.arange(slot_cap, dtype=jnp.int32)
     chosen = mine[:, None, :] & (slot_of[:, None, :] == slots[None, :, None])
@@ -116,11 +436,14 @@
     combine = jnp.where(chosen, weight[:, None, :], 0.0)
     expert_gate_up = w_gate_up[0]
     expert_down = w_down[0]
-    summed = lax.psum(partial_value.astype(jnp.bfloat16), "col").astype(jnp.float32)
-    stream = (residual.astype(jnp.float32) + summed).astype(jnp.bfloat16)
+    partial_value = partial_value.astype(jnp.bfloat16)
+    if in_kernels:
+        stream, gathered = spread(partial_value, residual, norm_gain, row_count)
+    else:
+        summed = lax.psum(partial_value, "col").astype(jnp.float32)
+        stream = (residual.astype(jnp.float32) + summed).astype(jnp.bfloat16)
+        gathered = lax.all_gather(normalize(stream, norm_gain), "row", axis=0, tiled=False)
     stream_part = lax.dynamic_slice_in_dim(stream, col_index * feature_count, feature_count, 1)
-    source_rows = normalize(stream, norm_gain)
-    gathered = lax.all_gather(source_rows, "row", axis=0, tiled=False)
     packed = jnp.einsum(
         "nst,ntd->nsd", selector, gathered, preferred_element_type=jnp.float32
     ).astype(jnp.bfloat16).reshape(row_count * slot_cap, -1)
@@ -131,9 +454,13 @@
     scaled = expert_partial.reshape(row_count, slot_cap, -1) * jnp.sum(combine, 2)[:, :, None]
     mixed = jnp.einsum(
         "nst,nsd->ntd", selector, scaled.astype(jnp.bfloat16), preferred_element_type=jnp.float32
-    ).astype(jnp.bfloat16).reshape(row_count * tok_rows, -1)
-    mixed = lax.psum_scatter(mixed, "row", scatter_dimension=0, tiled=True)
-    mixed = lax.psum_scatter(mixed, "col", scatter_dimension=1, tiled=True)
+    ).astype(jnp.bfloat16)
+    if in_kernels:
+        mixed = fold(mixed, row_count, feature_count)
+    else:
+        mixed = mixed.reshape(row_count * tok_rows, -1)
+        mixed = lax.psum_scatter(mixed, "row", scatter_dimension=0, tiled=True)
+        mixed = lax.psum_scatter(mixed, "col", scatter_dimension=1, tiled=True)
     return (stream_part.astype(jnp.float32) + mixed.astype(jnp.float32)).astype(jnp.bfloat16)
 
 

time: 269 us -> 155 us (0.58)
  waiting for transfers between devices: 163 us -> 0 us
  Pallas kernels: 0 us -> 103 us
  blocking collectives: 22.1 us -> 0 us
  starting transfers between devices: 19.1 us -> 0 us
  between operations: 13.4 us -> 0.2 us
    pallas_call x0 -> x3, Pallas kernels: none -> 103 us  [the longest x1 48.7 us: spread(): pl.pallas_call(lambda *refs: spread_kernel(rows, *refs), out_shape=(jax.S...]
    reduce_scatter x1 -> x0, waiting for transfers between devices: 82 us -> none  [local(): mixed = lax.psum_scatter(mixed, 'row', scatter_dimension=0, tiled=True)]
    all_gather x1 -> x0, waiting for transfers between devices: 37.7 us -> none  [local(): gathered = lax.all_gather(source_rows, 'row', axis=0, tiled=False)]
    psum x1 -> x0, waiting for transfers between devices: 26.4 us -> none  [local(): lax.psum(partial_value.astype(jnp.bfloat16), 'col').astype(jnp.float32)]
    all_gather x1 -> x0, blocking collectives: 22.1 us -> none  [local(): routing = lax.all_gather(routing, 'row', axis=0, tiled=False)]
    ppermute x6 -> x0, starting transfers between devices: 19 us -> none  [shifted(): return lax.ppermute(shard, axis, pairs)]
    unnamed x5 -> x0, waiting for transfers between devices: 16.4 us -> none
    unnamed x14 -> x4, local copies, waits for them, and re-layouts: 5.16 us -> 1.89 us
  transfers between devices with their start and end apart: 10 -> 0, of which waited for: 4 -> 0; matrix products, arithmetic and copies ran while one was open for 2% -> 0% of each run, Pallas kernels for 0% -> 0%
where the time goes in v2:
time: 155 us; the launch traced here: 154 us
  Pallas kernels  103 us (66%)
  matrix products  36.7 us (24%)
  local copies, waits for them, and re-layouts  7.12 us (5%)
  other arithmetic  6.72 us (4%)
    pallas_call x1, Pallas kernels, spread(): pl.pallas_call(lambda *refs: spread_kernel(rows, *refs), out_shape=(jax.S...  48.7 us
    pallas_call x1, Pallas kernels, fold(): pl.pallas_call(lambda *refs: fold_kernel(rows, *refs), out_shape=jax.Shap...  43 us
    pallas_call x1, Pallas kernels, halo(): pl.pallas_call(lambda *refs: halo_kernel(rows, shifts, *refs), out_shape=...  11.8 us
    dot_general x1, matrix products, local(): jnp.einsum('nst,nsd->ntd', selector, scaled.astype(jnp.bfloat16), preferr...  10.8 us
    dot_general x1, matrix products, local(): up = jnp.dot(packed, expert_gate_up[1], preferred_element_type=jnp.float32)  8.82 us
    dot_general x1, matrix products, local(): jnp.dot(packed, expert_gate_up[0], preferred_element_type=jnp.float32)  7.37 us
    dot_general x1, matrix products, local(): partial_value = jnp.dot(attended, w_out, preferred_element_type=jnp.float32)  4.41 us
    dot_general x1, matrix products, local(): jnp.einsum('nst,ntd->nsd', selector, gathered, preferred_element_type=jnp...  3.68 us

profile of v2, /device:TPU:0, one launch (start us, length us, event | category | flops | bytes accessed | tf_op | source)
XLA Modules:
  0.0 154.2 jit_solution(14734907215873781886)
XLA Ops:
  0.0 0.7 convert_element_type.52
  0.7 0.1 broadcast_compare_fusion
  0.7 0.7 max.18
  1.5 0.7 convert_element_type.51
  2.2 0.7 maximum_bitcast_fusion
  2.9 1.3 reshape.190.refs_2_
  4.2 0.8 constant_dynamic-slice_fusion.2
  5.0 11.8 %halo.1 = (bf16[2,64,512]{2,1,0:T(8,128)(2,1)S(1)}, f32[16,16,64]{2,1,0:T(8,128)S(1)}) custom-call(bf16[64,512]{1,0:T(8,128)(2,1)S(1)} %pad_maximum_fusion.2.refs_0_, f32[16,64]{1,0:T(8,128)S(1)} %pad_maximum_fusion.3.refs_1_), custom_call_target="tpu_custom_call" | custom-call | tf_op jit(solution)/shard_map/halo/pallas_call | solution.py:108
  16.9 0.7 pad_add_fusion.1
  17.6 0.2 reduce_window_sum.11
  17.9 0.1 select_reduce_fusion
  18.0 0.8 compare_and_fusion
  18.8 0.1 copy.17
  18.9 0.1 copy.16
  19.0 1.5 reshape.188
  20.5 0.0 copy-start
  20.5 0.6 fusion.37
  21.1 0.1 broadcast_maximum_fusion
  21.2 0.7 fusion.22
  21.8 0.1 exponential_add_fusion
  21.9 1.1 convolution_convert_fusion.3
  23.0 1.9 %copy-done = bf16[2048,2880]{0,1:T(8,128)(2,1)S(1)} copy-done((bf16[2048,2880]{0,1:T(8,128)(2,1)S(1)}, bf16[2048,2880]{0,1:T(8,128)(2,1)}, u32[]{:S(2)}) %copy-start) | copy-done | bytes 11796504
  24.9 4.4 %convolution_convert_fusion.2.refs_0_ = bf16[64,2880]{1,0:T(8,128)(2,1)} fusion(bf16[64,2048]{0,1:T(8,128)(2,1)S(1)} %bitcast.60, bf16[2048,2880]{0,1:T(8,128)(2,1)S(1)} %copy-done), kind=kOutput, calls=%fused_computation.11 | convolution fusion | flops 755159040 | bytes 12427264 | tf_op jit(solution)/shard_map/dot_general | solution.py:425
  29.3 48.7 %spread.1 = (bf16[64,2880]{1,0:T(8,128)(2,1)}, bf16[16,64,2880]{2,1,0:T(8,128)(2,1)}) custom-call(bf16[64,2880]{1,0:T(8,128)(2,1)} %convolution_convert_fusion.2.refs_0_, bf16[64,2880]{1,0:T(8,128)(2,1)} %refs_1_.1, f32[1,2880]{1,0:T(1,128)} %reshape.190.refs_2_), custom_call_target="tpu_custom_call" | custom-call | tf_op jit(solution)/shard_map/spread/pallas_call | solution.py:212
  78.0 3.7 %convolution_convert_fusion.1 = bf16[16,32,2880]{2,1,0:T(8,128)(2,1)S(1)} fusion(bf16[16,64,2880]{2,1,0:T(8,128)(2,1)} %get-tuple-element.12, s32[16,64]{1,0:T(8,128)S(1)} %broadcast_add_fusion, pred[16,64]{1,0:T(8,128)(4,1)S(1)} %reduce_or.9), kind=kOutput, calls=%fused_computation.10 | convolution fusion | flops 190283776 | bytes 8852480 | tf_op jit(solution)/shard_map/nst,ntd->nsd/dot_general | solution.py:447
  81.7 7.4 %fusion.2 = f32[512,1440]{0,1:T(8,128)S(1)} fusion(bf16[512,2880]{1,0:T(8,128)(2,1)S(1)} %bitcast.57, bf16[1,2,2880,1440]{2,3,1,0:T(8,128)(2,1)} %param.22), kind=kOutput, calls=%fused_computation.2 | convolution fusion | flops 4246732800 | bytes 14376960 | tf_op jit(solution)/shard_map/dot_general | solution.py:450
  89.0 8.8 %fusion.19 = bf16[512,1440]{0,1:T(8,128)(2,1)S(1)} fusion(f32[512,1440]{0,1:T(8,128)S(1)} %fusion.2, bf16[512,2880]{1,0:T(8,128)(2,1)S(1)} %bitcast.58, bf16[1,2,2880,1440]{2,3,1,0:T(8,128)(2,1)} %param.22), kind=kOutput, calls=%fused_computation.15 | convolution fusion | flops 4252631040 | bytes 15851520 | tf_op jit(solution)/shard_map/dot_general | solution.py:451
  97.9 0.7 copy.19
  98.6 10.8 %convolution_convert_fusion.refs_0_ = bf16[16,64,2880]{2,1,0:T(8,128)(2,1)} fusion(bf16[16,32,1440]{2,1,0:T(8,128)(2,1)S(1)} %bitcast.59, bf16[1,1440,2880]{2,1,0:T(8,128)(2,1)} %param.23, f32[16,32]{1,0:T(8,128)S(1)} %select_reduce_fusion, s32[16,64]{1,0:T(8,128)S(1)} %broadcast_add_fusion, pred[16,64]{1,0:T(8,128)(4,1)S(1)} %reduce_or.9), kind=kOutput, calls=%fused_computation.9 | convolution fusion | flops 4441440256 | bytes 15674368 | tf_op jit(solution)/shard_map/nst,nsd->ntd/dot_general | solution.py:455
  109.4 0.0 copy-start.1
  109.4 43.0 %fold.1 = f32[64,1440]{1,0:T(8,128)} custom-call(bf16[16,64,2880]{2,1,0:T(8,128)(2,1)} %convolution_convert_fusion.refs_0_), custom_call_target="tpu_custom_call" | custom-call | tf_op jit(solution)/shard_map/fold/pallas_call | solution.py:318
  152.4 0.0 copy-done.1
  152.4 1.8 %add_convert_fusion = bf16[64,1440]{1,0:T(8,128)(2,1)} fusion(f32[64,1440]{1,0:T(8,128)} %fold.1, bf16[64,2880]{1,0:T(8,128)(2,1)S(1)} %copy-done.1, s32[]{:T(128)S(6)} %select_n.30), kind=kLoop, calls=%fused_computation.22 | loop fusion | flops 276480 | bytes 737284 | tf_op jit(solution)/shard_map/convert_element_type | solution.py:464
  (16 shorter events, 0.2 us)
Async XLA Ops:
  20.5 4.4 %copy-start = (bf16[2048,2880]{0,1:T(8,128)(2,1)S(1)}, bf16[2048,2880]{0,1:T(8,128)(2,1)}, u32[]{:S(2)}) copy-start(bf16[2048,2880]{0,1:T(8,128)(2,1)} %param.18) | copy-start | bytes 35389444
  109.4 43.0 %copy-start.1 = (bf16[64,2880]{1,0:T(8,128)(2,1)S(1)}, bf16[64,2880]{1,0:T(8,128)(2,1)}, u32[]{:S(2)}) copy-start(bf16[64,2880]{1,0:T(8,128)(2,1)} %get-tuple-element.11) | copy-start | bytes 1105924

commit v3 on v2

--- a/solution.py
+++ b/solution.py
@@ -45,7 +45,7 @@
 
 MESH = pl.DeviceIdType.MESH
 VMEM = pl.BlockSpec(memory_space=pltpu.VMEM)
-HALVES = 2
+PIECES = 4
 VMEM_BYTES = 60 * 1024 * 1024
 
 
@@ -127,12 +127,20 @@
     )(kv, meta)
 
 
-def ring_halves(distance, half_way, way):
-    return range(HALVES) if distance < half_way else [way]
+def ring_pieces(distance, half_way, way):
+    if distance < half_way:
+        return [1, 2, 0]
+    return [1, 0] if way == 0 else [2]
+
+
+def piece_rows(index, size):
+    col = lax.axis_index("col")
+    start = (index + col * (PIECES - 1 - 2 * index)) * size
+    return pl.ds(pl.multiple_of(start, size), size)
 
 
 def spread_kernel(rows, partial_ref, residual_ref, gain_ref, stream_ref, out_ref, part_in,
-                  x_sem, send, recv, sib_send, sib_recv):
+                  x_sem, send, recv, over_send, over_recv, sib_send, sib_recv):
     chips = rows // 2
     half_way = chips // 2
     row = lax.axis_index("row")
@@ -146,63 +154,73 @@
     cross = remote(partial_ref, part_in, x_sem.at[0], x_sem.at[1], partner)
     cross.start()
     cross.wait()
-    size = partial_ref.shape[0] // HALVES
-    for half in range(HALVES):
-        at = pl.ds(half * size, size)
+    size = partial_ref.shape[0] // PIECES
+    for half in range(2):
+        at = pl.ds(half * 2 * size, 2 * size)
         summed = partial_ref[at, :].astype(jnp.float32) + part_in[at, :].astype(jnp.float32)
         stream = (residual_ref[at, :].astype(jnp.float32) + summed).astype(jnp.bfloat16)
         stream_ref[at, :] = stream
         out_ref[row, at, :] = normalize(stream, gain_ref[...])
 
-    def piece(source, half, which):
-        return out_ref.at[ring_row(place + source, chips, which), pl.ds(half * size, size)]
-
-    def hop(way, distance, half):
-        source = -distance if way == 0 else distance
-        back = source + (1 if way == 0 else -1)
-        return remote(piece(back, half, core), piece(back, half, core),
-                      send.at[way, distance - 1, half], recv.at[way, distance - 1, half], ways[way])
-
-    def landed(way, distance, half):
-        source = -distance if way == 0 else distance
-        return remote(piece(source, half, core), piece(source, half, core),
-                      send.at[way, distance - 1, half], recv.at[way, distance - 1, half], ways[way])
-
-    def pass_on(way, distance, half, which):
-        source = -distance if way == 0 else distance
-        return remote(piece(source, half, which), piece(source, half, which),
-                      sib_send.at[way, distance, half], sib_recv.at[way, distance, half], sibling)
+    def part(offset, index, which):
+        return out_ref.at[ring_row(place + offset, chips, which), piece_rows(index, size)]
+
+    def offset_of(way, distance):
+        return -distance if way == 0 else distance
+
+    def hop(way, distance, index, sending):
+        at = part(offset_of(way, distance - 1 if sending else distance), index, core)
+        return remote(at, at, send.at[way, distance - 1, index], recv.at[way, distance - 1, index],
+                      ways[way])
+
+    def over(way, distance, sending):
+        at = part(offset_of(way, distance), 0 if sending else PIECES - 1, core)
+        return remote(at, at, over_send.at[way, distance - 1], over_recv.at[way, distance - 1],
+                      partner)
+
+    def pass_on(way, distance, index, which):
+        at = part(offset_of(way, distance), index, which)
+        return remote(at, at, sib_send.at[way, distance, index], sib_recv.at[way, distance, index],
+                      sibling)
 
     sent = []
-    for half in range(HALVES):
-        for way in range(2):
-            if half in ring_halves(1, half_way, way):
-                copy = hop(way, 1, half)
-                copy.start()
-                sent.append(copy)
-        copy = pass_on(0, 0, half, core)
+
+    def go(copy):
         copy.start()
         sent.append(copy)
+
+    for index in [1, 2, 0]:
+        for way in range(2):
+            if index in ring_pieces(1, half_way, way):
+                go(hop(way, 1, index, True))
+    mine = out_ref.at[row]
+    theirs = out_ref.at[row + 1 - 2 * core]
+    go(remote(mine, mine, x_sem.at[2], x_sem.at[3], sibling))
     for distance in range(1, half_way + 1):
-        for half in range(HALVES):
+        for index in [1, 2, 0]:
             for way in range(2):
-                if half not in ring_halves(distance, half_way, way):
+                if index not in ring_pieces(distance, half_way, way):
                     continue
-                landed(way, distance, half).wait_recv()
-                if distance < half_way and half in ring_halves(distance + 1, half_way, way):
-                    copy = hop(way, distance + 1, half)
-                    copy.start()
-                    sent.append(copy)
-                copy = pass_on(way, distance, half, core)
-                copy.start()
-                sent.append(copy)
-    for half in range(HALVES):
-        pass_on(0, 0, half, 1 - core).wait_recv()
+                hop(way, distance, index, False).wait_recv()
+                if distance < half_way and index in ring_pieces(distance + 1, half_way, way):
+                    go(hop(way, distance + 1, index, True))
+                if index == 0:
+                    go(over(way, distance, True))
+                go(pass_on(way, distance, index, core))
+        for way in range(2):
+            if distance > 1 and 0 in ring_pieces(distance - 1, half_way, way):
+                over(way, distance - 1, False).wait_recv()
+                go(pass_on(way, distance - 1, PIECES - 1, core))
+    for way in range(2):
+        if 0 in ring_pieces(half_way, half_way, way):
+            over(way, half_way, False).wait_recv()
+            go(pass_on(way, half_way, PIECES - 1, core))
+    remote(theirs, theirs, x_sem.at[2], x_sem.at[3], sibling).wait_recv()
     for distance in range(1, half_way + 1):
-        for half in range(HALVES):
-            for way in range(2):
-                if half in ring_halves(distance, half_way, way):
-                    pass_on(way, distance, half, 1 - core).wait_recv()
+        for way in range(2):
+            indices = list(ring_pieces(distance, half_way, way))
+            for index in indices + ([PIECES - 1] if 0 in indices else []):
+                pass_on(way, distance, index, 1 - core).wait_recv()
     for copy in sent:
         copy.wait_send()
 
@@ -219,21 +237,23 @@
         out_specs=(VMEM, VMEM),
         scratch_shapes=[
             pltpu.VMEM(residual.shape, jnp.bfloat16),
-            pltpu.SemaphoreType.DMA((2,)),
-            pltpu.SemaphoreType.DMA((2, half_way, HALVES)),
-            pltpu.SemaphoreType.DMA((2, half_way, HALVES)),
-            pltpu.SemaphoreType.DMA((2, half_way + 1, HALVES)),
-            pltpu.SemaphoreType.DMA((2, half_way + 1, HALVES)),
+            pltpu.SemaphoreType.DMA((4,)),
+            pltpu.SemaphoreType.DMA((2, half_way, PIECES)),
+            pltpu.SemaphoreType.DMA((2, half_way, PIECES)),
+            pltpu.SemaphoreType.DMA((2, half_way)),
+            pltpu.SemaphoreType.DMA((2, half_way)),
+            pltpu.SemaphoreType.DMA((2, half_way + 1, PIECES)),
+            pltpu.SemaphoreType.DMA((2, half_way + 1, PIECES)),
         ],
         compiler_params=pltpu.CompilerParams(
-            collective_id=2, has_side_effects=True, vmem_limit_bytes=VMEM_BYTES
+            collective_id=2, has_side_effects=True, vmem_limit_bytes=VMEM_BYTES // 4
         ),
         name="spread",
     )(partial, residual, gain.reshape(1, -1))
 
 
-def fold_kernel(rows, part_ref, out_ref, sib_buf, ring_in, ring_out, x_out, x_in,
-                x_sem, send, recv, sib_send, sib_recv):
+def fold_kernel(rows, part_ref, out_ref, sib_buf, ring_in, ring_out, over_out, over_in, x_out, x_in,
+                x_sem, send, recv, over_send, over_recv, sib_send, sib_recv):
     chips = rows // 2
     half_way = chips // 2
     row = lax.axis_index("row")
@@ -254,57 +274,75 @@
                       sib_send.at[offset], sib_recv.at[offset], sibling)
         copy.start()
         shared[offset] = copy
-    size = part_ref.shape[1] // HALVES
+    size = part_ref.shape[1] // PIECES
     seen = set()
 
-    def own(offset, half):
+    def own(offset, index):
         if offset not in seen:
             shared[offset].wait_recv()
             seen.add(offset)
-        at = pl.ds(half * size, size)
+        at = piece_rows(index, size)
         return part_ref[ring_row(place + offset, chips, core), at, :].astype(
             jnp.float32
         ) + sib_buf[offset, at, :].astype(jnp.float32)
 
-    def hop(way, distance, half):
-        at = pl.ds(half * size, size)
+    def hop(way, distance, index):
+        at = pl.ds(index * size, size)
         return remote(ring_out.at[way, distance - 1, at], ring_in.at[way, distance - 1, at],
-                      send.at[way, distance - 1, half], recv.at[way, distance - 1, half], ways[way])
-
-    def arrived(way, distance, half):
-        hop(way, distance, half).wait_recv()
-        return ring_in[way, distance - 1, pl.ds(half * size, size), :].astype(jnp.float32)
+                      send.at[way, distance - 1, index], recv.at[way, distance - 1, index],
+                      ways[way])
+
+    def arrived(way, distance, index):
+        hop(way, distance, index).wait_recv()
+        return ring_in[way, distance - 1, pl.ds(index * size, size), :].astype(jnp.float32)
+
+    def over(offset):
+        return remote(over_out.at[offset], over_in.at[offset], over_send.at[offset],
+                      over_recv.at[offset], partner)
 
     sent = []
+
+    def go(copy):
+        copy.start()
+        sent.append(copy)
+
     for distance in range(half_way, 0, -1):
-        for half in range(HALVES):
+        for offset in sorted({distance, chips - distance}):
+            over_out[offset] = own(offset, PIECES - 1).astype(jnp.bfloat16)
+            go(over(offset))
+        for index in [1, 2, 0]:
             for way in range(2):
-                if half not in ring_halves(distance, half_way, way):
+                if index not in ring_pieces(distance, half_way, way):
                     continue
-                value = own(distance if way == 0 else chips - distance, half)
-                if distance < half_way and half in ring_halves(distance + 1, half_way, way):
-                    value = value + arrived(way, distance + 1, half)
-                ring_out[way, distance - 1, pl.ds(half * size, size), :] = value.astype(jnp.bfloat16)
-                copy = hop(way, distance, half)
-                copy.start()
-                sent.append(copy)
+                offset = distance if way == 0 else chips - distance
+                value = own(offset, index)
+                if index == 0:
+                    over(offset).wait_recv()
+                    value = value + over_in[offset].astype(jnp.float32)
+                if distance < half_way and index in ring_pieces(distance + 1, half_way, way):
+                    value = value + arrived(way, distance + 1, index)
+                ring_out[way, distance - 1, pl.ds(index * size, size), :] = value.astype(
+                    jnp.bfloat16
+                )
+                go(hop(way, distance, index))
     width = out_ref.shape[1]
     crosses = []
-    for half in range(HALVES):
-        at = pl.ds(half * size, size)
-        value = own(0, half)
+    for index in [3, 1, 2, 0]:
+        at = piece_rows(index, size)
+        value = own(0, index)
         for way in range(2):
-            if half in ring_halves(1, half_way, way):
-                value = value + arrived(way, 1, half)
+            if index in ring_pieces(1, half_way, way):
+                value = value + arrived(way, 1, index)
         low, high = value[:, :width], value[:, width:]
         x_out[at, :] = jnp.where(col == 0, high, low).astype(jnp.bfloat16)
         out_ref[at, :] = jnp.where(col == 0, low, high)
-        copy = remote(x_out.at[at], x_in.at[at], x_sem.at[0, half], x_sem.at[1, half], partner)
-        copy.start()
-        crosses.append(copy)
-    for half in range(HALVES):
-        at = pl.ds(half * size, size)
-        crosses[half].wait()
+        copy = remote(x_out.at[at], x_in.at[at], x_sem.at[0, index], x_sem.at[1, index], partner)
+        go(copy)
+    for index in [0, 2, 1, 3]:
+        at = piece_rows(index, size)
+        named = PIECES - 1 - index
+        remote(x_out.at[at], x_in.at[at], x_sem.at[0, named], x_sem.at[1, named],
+               partner).wait_recv()
         out_ref[at, :] += x_in[at, :].astype(jnp.float32)
     for copy in sent:
         copy.wait_send()
@@ -324,16 +362,20 @@
             pltpu.VMEM((rows // 2, *block), jnp.bfloat16),
             pltpu.VMEM((2, half_way, *block), jnp.bfloat16),
             pltpu.VMEM((2, half_way, *block), jnp.bfloat16),
+            pltpu.VMEM((rows // 2, block[0] // PIECES, block[1]), jnp.bfloat16),
+            pltpu.VMEM((rows // 2, block[0] // PIECES, block[1]), jnp.bfloat16),
             pltpu.VMEM((block[0], width), jnp.bfloat16),
             pltpu.VMEM((block[0], width), jnp.bfloat16),
-            pltpu.SemaphoreType.DMA((2, HALVES)),
-            pltpu.SemaphoreType.DMA((2, half_way, HALVES)),
-            pltpu.SemaphoreType.DMA((2, half_way, HALVES)),
+            pltpu.SemaphoreType.DMA((2, PIECES)),
+            pltpu.SemaphoreType.DMA((2, half_way, PIECES)),
+            pltpu.SemaphoreType.DMA((2, half_way, PIECES)),
+            pltpu.SemaphoreType.DMA((rows // 2,)),
+            pltpu.SemaphoreType.DMA((rows // 2,)),
             pltpu.SemaphoreType.DMA((rows // 2,)),
             pltpu.SemaphoreType.DMA((rows // 2,)),
         ],
         compiler_params=pltpu.CompilerParams(
-            collective_id=3, has_side_effects=True, vmem_limit_bytes=VMEM_BYTES
+            collective_id=3, has_side_effects=True, vmem_limit_bytes=VMEM_BYTES // 5 * 2
         ),
         name="fold",
     )(part)
@@ -372,7 +414,7 @@
     shift_count = (WINDOW + tok_rows - 2) // tok_rows
     block_bytes = 2 * residual.shape[0] * residual.shape[1]
     in_kernels = (
-        col_count == 2 and row_count % 4 == 0 and row_count >= 8
+        col_count == 2 and row_count % 4 == 0 and row_count >= 8 and tok_rows % 64 == 0
         and 4 * row_count * block_bytes < VMEM_BYTES
     )
     routing = jnp.concatenate([expert_ids.astype(jnp.float32), route_weight], 1).T

time: 155 us -> 136 us (0.88)
  Pallas kernels: 103 us -> 87.5 us
  matrix products: 36.7 us -> 33.3 us
  local copies, waits for them, and re-layouts: 7.12 us -> 9.22 us
    pallas_call x1, Pallas kernels: 43 us -> 34.1 us  [fold(): pl.pallas_call(lambda *refs: fold_kernel(rows, *refs), out_shape=jax.Shap...]
    pallas_call x1, Pallas kernels: 48.7 us -> 41.6 us  [spread(): pl.pallas_call(lambda *refs: spread_kernel(rows, *refs), out_shape=(jax.S...]
    dot_general x1, matrix products: 3.68 us -> 0.97 us  [local(): jnp.einsum('nst,ntd->nsd', selector, gathered, preferred_element_type=jnp...]
    unnamed x4 -> x6, local copies, waits for them, and re-layouts: 1.89 us -> 4.58 us
where the time goes in v3:
time: 136 us
  Pallas kernels  87.5 us (64%)
  matrix products  33.3 us (24%)
  local copies, waits for them, and re-layouts  9.22 us (7%)
  other arithmetic  5.73 us (4%)
    pallas_call x1, Pallas kernels, spread(): pl.pallas_call(lambda *refs: spread_kernel(rows, *refs), out_shape=(jax.S...  41.6 us
    pallas_call x1, Pallas kernels, fold(): pl.pallas_call(lambda *refs: fold_kernel(rows, *refs), out_shape=jax.Shap...  34.1 us
    pallas_call x1, Pallas kernels, halo(): pl.pallas_call(lambda *refs: halo_kernel(rows, shifts, *refs), out_shape=...  11.8 us
    dot_general x1, matrix products, local(): jnp.einsum('nst,nsd->ntd', selector, scaled.astype(jnp.bfloat16), preferr...  10.8 us
    dot_general x1, matrix products, local(): up = jnp.dot(packed, expert_gate_up[1], preferred_element_type=jnp.float32)  8.82 us
    dot_general x1, matrix products, local(): jnp.dot(packed, expert_gate_up[0], preferred_element_type=jnp.float32)  7.37 us
    unnamed x6, local copies, waits for them, and re-layouts  4.58 us
    dot_general x1, matrix products, local(): partial_value = jnp.dot(attended, w_out, preferred_element_type=jnp.float32)  3.67 us

profile of v3, /device:TPU:0, one launch (start us, length us, event | category | flops | bytes accessed | tf_op | source)
XLA Modules:
  0.0 136.0 jit_solution(13008838872670950917)
XLA Ops:
  0.0 0.7 convert_element_type.52
  0.7 0.1 broadcast_compare_fusion
  0.7 0.7 max.18
  1.5 0.7 convert_element_type.51
  2.2 0.7 maximum_bitcast_fusion
  2.9 0.7 reshape.190.refs_2_
  3.6 0.8 constant_dynamic-slice_fusion.2
  4.4 11.8 %halo.1 = (bf16[2,64,512]{2,1,0:T(8,128)(2,1)S(1)}, f32[16,16,64]{2,1,0:T(8,128)S(1)}) custom-call(bf16[64,512]{1,0:T(8,128)(2,1)S(1)} %pad_maximum_fusion.2.refs_0_, f32[16,64]{1,0:T(8,128)S(1)} %pad_maximum_fusion.3.refs_1_), custom_call_target="tpu_custom_call" | custom-call | tf_op jit(solution)/shard_map/halo/pallas_call | solution.py:108
  16.3 0.7 pad_add_fusion.1
  17.0 0.2 reduce_window_sum.11
  17.3 0.1 select_reduce_fusion
  17.4 0.8 compare_and_fusion
  18.2 0.1 copy.17
  18.3 0.1 copy.16
  18.4 1.5 %reshape.188 = bf16[64,4,8,64]{3,2,1,0:T(8,128)(2,1)S(1)} reshape(bf16[64,2048]{1,0:T(8,128)(2,1)} %param.13) | data formatting | bytes 524288 | tf_op jit(solution)/shard_map/reshape | solution.py:462
  19.9 0.0 copy-start.2
  19.9 0.6 fusion.37
  20.5 0.1 broadcast_maximum_fusion
  20.6 0.7 fusion.22
  21.2 0.1 exponential_add_fusion
  21.3 1.1 convolution_convert_fusion.3
  22.4 1.9 %copy-done.2 = bf16[2048,2880]{0,1:T(8,128)(2,1)S(1)} copy-done((bf16[2048,2880]{0,1:T(8,128)(2,1)S(1)}, bf16[2048,2880]{0,1:T(8,128)(2,1)}, u32[]{:S(2)}) %copy-start.2) | copy-done | bytes 11796504
  24.3 0.0 copy-start.1
  24.3 3.7 %convolution_convert_fusion.2.refs_0_ = bf16[64,2880]{1,0:T(8,128)(2,1)S(1)} fusion(bf16[64,2048]{0,1:T(8,128)(2,1)S(1)} %bitcast.60, bf16[2048,2880]{0,1:T(8,128)(2,1)S(1)} %copy-done.2), kind=kOutput, calls=%fused_computation.11 | convolution fusion | flops 755159040 | bytes 12427264 | tf_op jit(solution)/shard_map/dot_general | solution.py:467
  27.9 0.0 copy-done.1
  28.0 41.6 %spread.1 = (bf16[64,2880]{1,0:T(8,128)(2,1)S(1)}, bf16[16,64,2880]{2,1,0:T(8,128)(2,1)S(1)}) custom-call(bf16[64,2880]{1,0:T(8,128)(2,1)S(1)} %convolution_convert_fusion.2.refs_0_, bf16[64,2880]{1,0:T(8,128)(2,1)S(1)} %copy-done.1, f32[1,2880]{1,0:T(1,128)S(1)} %reshape.190.refs_2_), custom_call_target="tpu_custom_call" | custom-call | tf_op jit(solution)/shard_map/spread/pallas_call | solution.py:230
  69.6 1.0 convolution_convert_fusion.1
  70.6 7.4 %fusion.2 = f32[512,1440]{0,1:T(8,128)S(1)} fusion(bf16[512,2880]{1,0:T(8,128)(2,1)S(1)} %bitcast.57, bf16[1,2,2880,1440]{2,3,1,0:T(8,128)(2,1)} %param.22), kind=kOutput, calls=%fused_computation.2 | convolution fusion | flops 4246732800 | bytes 14376960 | tf_op jit(solution)/shard_map/dot_general | solution.py:492
  77.9 8.8 %fusion.19 = bf16[512,1440]{0,1:T(8,128)(2,1)S(1)} fusion(f32[512,1440]{0,1:T(8,128)S(1)} %fusion.2, bf16[512,2880]{1,0:T(8,128)(2,1)S(1)} %bitcast.58, bf16[1,2,2880,1440]{2,3,1,0:T(8,128)(2,1)} %param.22), kind=kOutput, calls=%fused_computation.15 | convolution fusion | flops 4252631040 | bytes 15851520 | tf_op jit(solution)/shard_map/dot_general | solution.py:493
  86.8 0.7 copy.19
  87.5 10.8 %convolution_convert_fusion.refs_0_ = bf16[16,64,2880]{2,1,0:T(8,128)(2,1)} fusion(bf16[16,32,1440]{2,1,0:T(8,128)(2,1)S(1)} %bitcast.59, bf16[1,1440,2880]{2,1,0:T(8,128)(2,1)} %param.23, f32[16,32]{1,0:T(8,128)S(1)} %select_reduce_fusion, s32[16,64]{1,0:T(8,128)S(1)} %broadcast_add_fusion, pred[16,64]{1,0:T(8,128)(4,1)S(1)} %reduce_or.9), kind=kOutput, calls=%fused_computation.9 | convolution fusion | flops 4441440256 | bytes 15674368 | tf_op jit(solution)/shard_map/nst,nsd->ntd/dot_general | solution.py:497
  98.3 0.0 copy-start
  98.3 2.7 %copy-done = bf16[16,64,2880]{2,1,0:T(8,128)(2,1)S(1)} copy-done((bf16[16,64,2880]{2,1,0:T(8,128)(2,1)S(1)}, bf16[16,64,2880]{2,1,0:T(8,128)(2,1)}, u32[]{:S(2)}) %copy-start) | copy-done | bytes 5898264
  101.0 34.1 %fold.1 = f32[64,1440]{1,0:T(8,128)S(1)} custom-call(bf16[16,64,2880]{2,1,0:T(8,128)(2,1)S(1)} %copy-done), custom_call_target="tpu_custom_call" | custom-call | tf_op jit(solution)/shard_map/fold/pallas_call | solution.py:356
  135.1 0.8 add_convert_fusion
  (16 shorter events, 0.2 us)
Async XLA Ops:
  19.9 4.4 %copy-start.2 = (bf16[2048,2880]{0,1:T(8,128)(2,1)S(1)}, bf16[2048,2880]{0,1:T(8,128)(2,1)}, u32[]{:S(2)}) copy-start(bf16[2048,2880]{0,1:T(8,128)(2,1)} %param.18) | copy-start | bytes 35389444
  24.3 3.7 %copy-start.1 = (bf16[64,2880]{1,0:T(8,128)(2,1)S(1)}, bf16[64,2880]{1,0:T(8,128)(2,1)}, u32[]{:S(2)}) copy-start(bf16[64,2880]{1,0:T(8,128)(2,1)} %refs_1_.1) | copy-start | bytes 1105924
  98.3 2.7 %copy-start = (bf16[16,64,2880]{2,1,0:T(8,128)(2,1)S(1)}, bf16[16,64,2880]{2,1,0:T(8,128)(2,1)}, u32[]{:S(2)}) copy-start(bf16[16,64,2880]{2,1,0:T(8,128)(2,1)} %convolution_convert_fusion.refs_0_) | copy-start | bytes 17694724

commit v4 on v3

--- a/solution.py
+++ b/solution.py
@@ -75,56 +75,48 @@
     )
 
 
-def halo_kernel(rows, shifts, kv_ref, meta_ref, kv_out, meta_out, kv_send, kv_recv, m_send, m_recv, l_sem):
+def halo_kernel(rows, shifts, key_ref, value_ref, segment_ref, key_out, value_out, segment_out, send, recv):
     row = lax.axis_index("row")
-    others = [{"row": lax.rem(row + step, rows)} for step in range(1, rows)]
-    greet(others)
+    col = lax.axis_index("col")
+    after = [{"row": lax.rem(row + shift, rows)} for shift in range(1, shifts + 1)]
+    before = [{"row": lax.rem(row + rows - shift, rows)} for shift in range(1, shifts + 1)]
+    greet(after + before)
+    width = key_out.shape[2]
+    lanes = pl.ds(pl.multiple_of(col * width, width), width)
     copies = []
-    for shift in range(1, shifts + 1):
-        copies.append(
-            remote(kv_ref, kv_out.at[shift - 1], kv_send.at[shift - 1], kv_recv.at[shift - 1],
-                   others[shift - 1])
-        )
-    for step in range(1, rows):
-        copies.append(
-            remote(meta_ref, meta_out.at[row], m_send.at[step - 1], m_recv.at[step - 1],
-                   others[step - 1])
-        )
+    for at in range(shifts):
+        for which, (src, dst) in enumerate([
+            (segment_ref, segment_out.at[at]),
+            (key_ref.at[:, lanes], key_out.at[at]),
+            (value_ref.at[:, lanes], value_out.at[at]),
+        ]):
+            copies.append(remote(src, dst, send.at[at, which], recv.at[at, which], after[at]))
     for copy in copies:
         copy.start()
-    mine = pltpu.make_async_copy(meta_ref, meta_out.at[row], l_sem)
-    mine.start()
-    for shift in range(1, shifts + 1):
-        copies[shift - 1].wait()
-    for step in range(1, rows):
-        copies[shifts + step - 1].wait_send()
-        source = lax.rem(row - step + rows, rows)
-        remote(meta_ref, meta_out.at[source], m_send.at[step - 1], m_recv.at[step - 1],
-               others[step - 1]).wait_recv()
-    mine.wait()
-
-
-def halo(kv, meta, rows, shifts):
+    for copy in copies:
+        copy.wait()
+
+
+def halo(keys, values, segments, rows, shifts, width):
+    tokens = keys.shape[0]
     return pl.pallas_call(
         lambda *refs: halo_kernel(rows, shifts, *refs),
         out_shape=(
-            jax.ShapeDtypeStruct((shifts, *kv.shape), kv.dtype),
-            jax.ShapeDtypeStruct((rows, *meta.shape), meta.dtype),
+            jax.ShapeDtypeStruct((shifts, tokens, width), keys.dtype),
+            jax.ShapeDtypeStruct((shifts, tokens, width), values.dtype),
+            jax.ShapeDtypeStruct((shifts, 1, tokens), segments.dtype),
         ),
-        in_specs=[VMEM] * 2,
-        out_specs=(VMEM, VMEM),
+        in_specs=[VMEM] * 3,
+        out_specs=(VMEM,) * 3,
         scratch_shapes=[
-            pltpu.SemaphoreType.DMA((shifts,)),
-            pltpu.SemaphoreType.DMA((shifts,)),
-            pltpu.SemaphoreType.DMA((rows,)),
-            pltpu.SemaphoreType.DMA((rows,)),
-            pltpu.SemaphoreType.DMA,
+            pltpu.SemaphoreType.DMA((shifts, 3)),
+            pltpu.SemaphoreType.DMA((shifts, 3)),
         ],
         compiler_params=pltpu.CompilerParams(
             collective_id=1, has_side_effects=True, vmem_limit_bytes=16 * 1024 * 1024
         ),
         name="halo",
-    )(kv, meta)
+    )(keys, values, segments.reshape(1, -1))
 
 
 def ring_pieces(distance, half_way, way):
@@ -139,8 +131,8 @@
     return pl.ds(pl.multiple_of(start, size), size)
 
 
-def spread_kernel(rows, partial_ref, residual_ref, gain_ref, stream_ref, out_ref, part_in,
-                  x_sem, send, recv, over_send, over_recv, sib_send, sib_recv):
+def spread_kernel(rows, partial_ref, residual_ref, gain_ref, meta_ref, stream_ref, out_ref, meta_out, part_in,
+                  x_sem, c_send, c_recv, m_send, m_recv, n_send, n_recv, l_sem, send, recv, over_send, over_recv, sib_send, sib_recv):
     chips = rows // 2
     half_way = chips // 2
     row = lax.axis_index("row")
@@ -151,12 +143,21 @@
     partner = {"col": 1 - col}
     ways = [{"row": ring_row(place + 1, chips, core)}, {"row": ring_row(place - 1, chips, core)}]
     greet([sibling, partner] + ways)
-    cross = remote(partial_ref, part_in, x_sem.at[0], x_sem.at[1], partner)
-    cross.start()
-    cross.wait()
     size = partial_ref.shape[0] // PIECES
-    for half in range(2):
-        at = pl.ds(half * 2 * size, 2 * size)
+    crosses = {}
+    for index in [2, 1, 3, 0]:
+        at = piece_rows(index, size)
+        named = PIECES - 1 - index
+        crosses[index] = remote(partial_ref.at[at], part_in.at[at], c_send.at[named],
+                                c_recv.at[named], partner)
+        crosses[index].start()
+    local_meta = pltpu.make_async_copy(meta_ref, meta_out.at[row], l_sem)
+    local_meta.start()
+
+    def ready(index):
+        at = piece_rows(index, size)
+        remote(partial_ref.at[at], part_in.at[at], c_send.at[index], c_recv.at[index],
+               partner).wait_recv()
         summed = partial_ref[at, :].astype(jnp.float32) + part_in[at, :].astype(jnp.float32)
         stream = (residual_ref[at, :].astype(jnp.float32) + summed).astype(jnp.bfloat16)
         stream_ref[at, :] = stream
@@ -190,12 +191,29 @@
         sent.append(copy)
 
     for index in [1, 2, 0]:
+        ready(index)
         for way in range(2):
             if index in ring_pieces(1, half_way, way):
                 go(hop(way, 1, index, True))
+    ready(PIECES - 1)
+    local_meta.wait()
+
+    def routing_hop(way, distance, sending):
+        back = offset_of(way, distance - 1 if sending else distance)
+        at = meta_out.at[ring_row(place + back, chips, core)]
+        return remote(at, at, m_send.at[way, distance - 1], m_recv.at[way, distance - 1], ways[way])
+
+    def routing_on(way, distance, which):
+        at = meta_out.at[ring_row(place + offset_of(way, distance), chips, which)]
+        return remote(at, at, n_send.at[way, distance], n_recv.at[way, distance], sibling)
+
+    reach = [half_way, half_way - 1]
+    for way in range(2):
+        go(routing_hop(way, 1, True))
+    go(routing_on(0, 0, core))
     mine = out_ref.at[row]
     theirs = out_ref.at[row + 1 - 2 * core]
-    go(remote(mine, mine, x_sem.at[2], x_sem.at[3], sibling))
+    go(remote(mine, mine, x_sem.at[0], x_sem.at[1], sibling))
     for distance in range(1, half_way + 1):
         for index in [1, 2, 0]:
             for way in range(2):
@@ -208,6 +226,12 @@
                     go(over(way, distance, True))
                 go(pass_on(way, distance, index, core))
         for way in range(2):
+            if distance <= reach[way]:
+                routing_hop(way, distance, False).wait_recv()
+                if distance < reach[way]:
+                    go(routing_hop(way, distance + 1, True))
+                go(routing_on(way, distance, core))
+        for way in range(2):
             if distance > 1 and 0 in ring_pieces(distance - 1, half_way, way):
                 over(way, distance - 1, False).wait_recv()
                 go(pass_on(way, distance - 1, PIECES - 1, core))
@@ -215,7 +239,12 @@
         if 0 in ring_pieces(half_way, half_way, way):
             over(way, half_way, False).wait_recv()
             go(pass_on(way, half_way, PIECES - 1, core))
-    remote(theirs, theirs, x_sem.at[2], x_sem.at[3], sibling).wait_recv()
+    remote(theirs, theirs, x_sem.at[0], x_sem.at[1], sibling).wait_recv()
+    for way in range(2):
+        for distance in range(way, reach[way] + 1):
+            routing_on(way, distance, 1 - core).wait_recv()
+    for index in range(PIECES):
+        crosses[index].wait_send()
     for distance in range(1, half_way + 1):
         for way in range(2):
             indices = list(ring_pieces(distance, half_way, way))
@@ -225,19 +254,27 @@
         copy.wait_send()
 
 
-def spread(partial, residual, gain, rows):
+def spread(partial, residual, gain, meta, rows):
     half_way = rows // 4
     return pl.pallas_call(
         lambda *refs: spread_kernel(rows, *refs),
         out_shape=(
             jax.ShapeDtypeStruct(residual.shape, jnp.bfloat16),
             jax.ShapeDtypeStruct((rows, *residual.shape), jnp.bfloat16),
+            jax.ShapeDtypeStruct((rows, *meta.shape), meta.dtype),
         ),
-        in_specs=[VMEM] * 3,
-        out_specs=(VMEM, VMEM),
+        in_specs=[VMEM] * 4,
+        out_specs=(VMEM,) * 3,
         scratch_shapes=[
             pltpu.VMEM(residual.shape, jnp.bfloat16),
-            pltpu.SemaphoreType.DMA((4,)),
+            pltpu.SemaphoreType.DMA((2,)),
+            pltpu.SemaphoreType.DMA((PIECES,)),
+            pltpu.SemaphoreType.DMA((PIECES,)),
+            pltpu.SemaphoreType.DMA((2, half_way)),
+            pltpu.SemaphoreType.DMA((2, half_way)),
+            pltpu.SemaphoreType.DMA((2, half_way + 1)),
+            pltpu.SemaphoreType.DMA((2, half_way + 1)),
+            pltpu.SemaphoreType.DMA,
             pltpu.SemaphoreType.DMA((2, half_way, PIECES)),
             pltpu.SemaphoreType.DMA((2, half_way, PIECES)),
             pltpu.SemaphoreType.DMA((2, half_way)),
@@ -249,7 +286,7 @@
             collective_id=2, has_side_effects=True, vmem_limit_bytes=VMEM_BYTES // 4
         ),
         name="spread",
-    )(partial, residual, gain.reshape(1, -1))
+    )(partial, residual, gain.reshape(1, -1), meta)
 
 
 def fold_kernel(rows, part_ref, out_ref, sib_buf, ring_in, ring_out, over_out, over_in, x_out, x_in,
@@ -415,6 +452,7 @@
     block_bytes = 2 * residual.shape[0] * residual.shape[1]
     in_kernels = (
         col_count == 2 and row_count % 4 == 0 and row_count >= 8 and tok_rows % 64 == 0
+        and kv_width % 128 == 0 and kv_width * col_count == key_states.shape[1]
         and 4 * row_count * block_bytes < VMEM_BYTES
     )
     routing = jnp.concatenate([expert_ids.astype(jnp.float32), route_weight], 1).T
@@ -423,22 +461,15 @@
     segment_parts = []
     start_parts = []
     if in_kernels:
-        own_pair = jnp.concatenate([own_keys, own_values], 1)
-        meta = jnp.concatenate(
-            [routing, jnp.broadcast_to(segment_ids.astype(jnp.float32)[None], (8, tok_rows))], 0
+        keys_before, values_before, segments_before = halo(
+            key_states, value_states, segment_ids, row_count, shift_count, kv_width
         )
-        pairs, metas = halo(own_pair, meta, row_count, shift_count)
-        routing = metas[:, : 2 * TOP]
-        all_segments = metas[:, 2 * TOP].astype(jnp.int32)
-    else:
-        routing = lax.all_gather(routing, "row", axis=0, tiled=False)
     for offset in range(shift_count, 0, -1):
         if in_kernels:
-            before = lax.rem(row_index - offset + row_count, row_count)
             arrived = (
-                pairs[offset - 1][:, :kv_width],
-                pairs[offset - 1][:, kv_width:],
-                lax.dynamic_index_in_dim(all_segments, before, 0, keepdims=False),
+                keys_before[offset - 1],
+                values_before[offset - 1],
+                segments_before[offset - 1, 0],
             )
         else:
             arrived = shifted((own_keys, own_values, segment_ids), "row", offset)
@@ -468,6 +499,17 @@
     feature_count = residual.shape[1] // col_count
     experts_all = w_gate_up.shape[0] * row_count
     slot_cap = max(2, 2 * TOP * tok_rows // experts_all)
+    expert_gate_up = w_gate_up[0]
+    expert_down = w_down[0]
+    partial_value = partial_value.astype(jnp.bfloat16)
+    if in_kernels:
+        stream, gathered, routing = spread(partial_value, residual, norm_gain, routing, row_count)
+    else:
+        summed = lax.psum(partial_value, "col").astype(jnp.float32)
+        stream = (residual.astype(jnp.float32) + summed).astype(jnp.bfloat16)
+        gathered = lax.all_gather(normalize(stream, norm_gain), "row", axis=0, tiled=False)
+        routing = lax.all_gather(routing, "row", axis=0, tiled=False)
+    stream_part = lax.dynamic_slice_in_dim(stream, col_index * feature_count, feature_count, 1)
     names_mine = routing[:, :TOP] == row_index.astype(jnp.float32)
     mine = jnp.any(names_mine, axis=1)
     weight = jnp.sum(jnp.where(names_mine, routing[:, TOP:], 0.0), axis=1)
@@ -476,16 +518,6 @@
     chosen = mine[:, None, :] & (slot_of[:, None, :] == slots[None, :, None])
     selector = chosen.astype(jnp.bfloat16)
     combine = jnp.where(chosen, weight[:, None, :], 0.0)
-    expert_gate_up = w_gate_up[0]
-    expert_down = w_down[0]
-    partial_value = partial_value.astype(jnp.bfloat16)
-    if in_kernels:
-        stream, gathered = spread(partial_value, residual, norm_gain, row_count)
-    else:
-        summed = lax.psum(partial_value, "col").astype(jnp.float32)
-        stream = (residual.astype(jnp.float32) + summed).astype(jnp.bfloat16)
-        gathered = lax.all_gather(normalize(stream, norm_gain), "row", axis=0, tiled=False)
-    stream_part = lax.dynamic_slice_in_dim(stream, col_index * feature_count, feature_count, 1)
     packed = jnp.einsum(
         "nst,ntd->nsd", selector, gathered, preferred_element_type=jnp.float32
     ).astype(jnp.bfloat16).reshape(row_count * slot_cap, -1)

time: 136 us -> 134 us (0.985)
  Pallas kernels: 87.5 us -> 78.6 us
  local copies, waits for them, and re-layouts: 9.22 us -> 14.4 us
  matrix products: 33.3 us -> 36.3 us
  other arithmetic: 5.73 us -> 3.71 us
    pallas_call x1, Pallas kernels: 41.6 us -> 36.3 us  [spread(): pl.pallas_call(lambda *refs: spread_kernel(rows, *refs), out_shape=(jax.S...]
    unnamed x6 -> x14, local copies, waits for them, and re-layouts: 4.58 us -> 9.25 us
    dot_general x1, matrix products: 0.97 us -> 3.68 us  [local(): jnp.einsum('nst,ntd->nsd', selector, gathered, preferred_element_type=jnp...]
    pallas_call x1, Pallas kernels: 11.8 us -> 9.6 us  [halo(): pl.pallas_call(lambda *refs: halo_kernel(rows, shifts, *refs), out_shape=...]
    pallas_call x1, Pallas kernels: 34.1 us -> 32.7 us  [fold(): pl.pallas_call(lambda *refs: fold_kernel(rows, *refs), out_shape=jax.Shap...]
where the time goes in v4:
time: 134 us; the launch traced here: 133 us
  Pallas kernels  78.6 us (59%)
  matrix products  36.3 us (27%)
  local copies, waits for them, and re-layouts  14.4 us (11%)
  other arithmetic  3.71 us (3%)
    pallas_call x1, Pallas kernels, spread(): pl.pallas_call(lambda *refs: spread_kernel(rows, *refs), out_shape=(jax.S...  36.3 us
    pallas_call x1, Pallas kernels, fold(): pl.pallas_call(lambda *refs: fold_kernel(rows, *refs), out_shape=jax.Shap...  32.7 us
    dot_general x1, matrix products, local(): jnp.einsum('nst,nsd->ntd', selector, scaled.astype(jnp.bfloat16), preferr...  11 us
    pallas_call x1, Pallas kernels, halo(): pl.pallas_call(lambda *refs: halo_kernel(rows, shifts, *refs), out_shape=...  9.6 us
    unnamed x14, local copies, waits for them, and re-layouts  9.25 us
    dot_general x1, matrix products, local(): up = jnp.dot(packed, expert_gate_up[1], preferred_element_type=jnp.float32)  8.82 us
    dot_general x1, matrix products, local(): jnp.dot(packed, expert_gate_up[0], preferred_element_type=jnp.float32)  7.2 us
    dot_general x1, matrix products, local(): jnp.einsum('nst,ntd->nsd', selector, gathered, preferred_element_type=jnp...  3.68 us

profile of v4, /device:TPU:0, one launch (start us, length us, event | category | flops | bytes accessed | tf_op | source)
XLA Modules:
  0.0 133.1 jit_solution(16431376409672030419)
XLA Ops:
  0.0 0.1 broadcast_compare_fusion
  0.1 0.7 max.18
  0.8 0.7 convert_element_type.48
  1.5 0.7 maximum_bitcast_fusion.4.refs_3_
  2.2 0.7 reshape.192.refs_2_
  2.9 0.8 constant_dynamic-slice_fusion
  3.7 0.1 copy.23
  3.8 0.1 copy.20
  3.9 0.0 copy-start.3
  4.0 0.8 copy-done.3
  4.8 0.0 copy-start.4
  4.8 0.8 copy-done.4
  5.6 0.0 copy-start.5
  5.6 0.7 copy-done.5
  6.3 9.6 %halo.1 = (bf16[2,64,256]{2,1,0:T(8,128)(2,1)S(1)}, bf16[2,64,256]{2,1,0:T(8,128)(2,1)S(1)}, s32[2,1,64]{2,1,0:T(1,128)S(1)}) custom-call(bf16[64,512]{1,0:T(8,128)(2,1)S(1)} %copy-done.3, bf16[64,512]{1,0:T(8,128)(2,1)S(1)} %copy-done.4, s32[1,64]{1,0:T(1,128)S(1)} %bitcast.60), custom_call_target="tpu_custom_call" | custom-call | tf_op jit(solution)/shard_map/halo/pallas_call | solution.py:102
  15.9 0.1 pad_add_fusion.1
  16.0 0.1 compare_and_fusion
  16.1 0.1 copy.30
  16.2 0.1 copy.31
  16.3 0.1 copy.33
  16.5 0.1 copy.32
  16.6 1.5 %reshape.190 = bf16[64,4,8,64]{3,2,1,0:T(8,128)(2,1)S(1)} reshape(bf16[64,2048]{1,0:T(8,128)(2,1)} %param.13) | data formatting | bytes 524288 | tf_op jit(solution)/shard_map/reshape | solution.py:493
  18.1 0.0 copy-start.6
  18.1 0.6 fusion.45
  18.7 0.1 broadcast_maximum_fusion
  18.8 0.7 fusion.22
  19.5 0.1 exponential_add_fusion
  19.6 1.2 convolution_convert_fusion.3
  20.8 1.6 %copy-done.6 = bf16[2048,2880]{0,1:T(8,128)(2,1)S(1)} copy-done((bf16[2048,2880]{0,1:T(8,128)(2,1)S(1)}, bf16[2048,2880]{0,1:T(8,128)(2,1)}, u32[]{:S(2)}) %copy-start.6) | copy-done | bytes 11796504
  22.4 0.0 copy-start.2
  22.4 3.7 %convolution_convert_fusion.2.refs_0_ = bf16[64,2880]{1,0:T(8,128)(2,1)S(1)} fusion(bf16[64,2048]{0,1:T(8,128)(2,1)S(1)} %bitcast.64, bf16[2048,2880]{0,1:T(8,128)(2,1)S(1)} %copy-done.6), kind=kOutput, calls=%fused_computation.11 | convolution fusion | flops 755159040 | bytes 12427264 | tf_op jit(solution)/shard_map/dot_general | solution.py:498
  26.1 0.0 copy-done.2
  26.1 36.3 %spread.1 = (bf16[64,2880]{1,0:T(8,128)(2,1)S(1)}, bf16[16,64,2880]{2,1,0:T(8,128)(2,1)S(1)}, f32[16,8,64]{2,1,0:T(8,128)S(1)}) custom-call(bf16[64,2880]{1,0:T(8,128)(2,1)S(1)} %convolution_convert_fusion.2.refs_0_, bf16[64,2880]{1,0:T(8,128)(2,1)S(1)} %copy-done.2, f32[1,2880]{1,0:T(1,128)S(1)} %reshape.192.refs_2_, f32[8,64]{1,0:T(8,128)S(1)} %maximum_bitcast_fusion.4.refs_3_), custom_call_target="tpu_custom_call" | custom-call | tf_op jit(solution)/shard_map/spread/pallas_call | solution.py:259
  62.5 0.0 copy-start.1
  62.5 2.6 %copy-done.1 = bf16[16,64,2880]{2,1,0:T(8,128)(2,1)} copy-done((bf16[16,64,2880]{2,1,0:T(8,128)(2,1)}, bf16[16,64,2880]{2,1,0:T(8,128)(2,1)S(1)}, u32[]{:S(2)}) %copy-start.1) | copy-done | bytes 5898264
  65.1 0.2 reduce_window_sum.11
  65.3 3.7 %convolution_convert_fusion.1 = bf16[16,32,2880]{2,1,0:T(8,128)(2,1)S(1)} fusion(bf16[16,64,2880]{2,1,0:T(8,128)(2,1)} %copy-done.1, s32[16,64]{1,0:T(8,128)S(1)} %broadcast_add_fusion, pred[16,64]{1,0:T(8,128)(4,1)S(1)} %reduce_or.9), kind=kOutput, calls=%fused_computation.10 | convolution fusion | flops 190283776 | bytes 8852480 | tf_op jit(solution)/shard_map/nst,ntd->nsd/dot_general | solution.py:521
  69.0 0.1 select_reduce_fusion
  69.2 7.2 %fusion.2 = f32[512,1440]{0,1:T(8,128)S(1)} fusion(bf16[512,2880]{1,0:T(8,128)(2,1)S(1)} %bitcast.61, bf16[1,2,2880,1440]{2,3,1,0:T(8,128)(2,1)} %param.22), kind=kOutput, calls=%fused_computation.2 | convolution fusion | flops 4246732800 | bytes 14376960 | tf_op jit(solution)/shard_map/dot_general | solution.py:524
  76.4 8.8 %fusion.19 = bf16[512,1440]{0,1:T(8,128)(2,1)S(1)} fusion(f32[512,1440]{0,1:T(8,128)S(1)} %fusion.2, bf16[512,2880]{1,0:T(8,128)(2,1)S(1)} %bitcast.62, bf16[1,2,2880,1440]{2,3,1,0:T(8,128)(2,1)} %param.22), kind=kOutput, calls=%fused_computation.15 | convolution fusion | flops 4252631040 | bytes 15851520 | tf_op jit(solution)/shard_map/dot_general | solution.py:525
  85.2 0.7 copy.27
  85.9 11.0 %convolution_convert_fusion.refs_0_ = bf16[16,64,2880]{2,1,0:T(8,128)(2,1)} fusion(bf16[16,32,1440]{2,1,0:T(8,128)(2,1)S(1)} %bitcast.63, bf16[1,1440,2880]{2,1,0:T(8,128)(2,1)} %param.23, f32[16,32]{1,0:T(8,128)S(1)} %select_reduce_fusion, s32[16,64]{1,0:T(8,128)S(1)} %broadcast_add_fusion, pred[16,64]{1,0:T(8,128)(4,1)S(1)} %reduce_or.9), kind=kOutput, calls=%fused_computation.9 | convolution fusion | flops 4441440256 | bytes 15674368 | tf_op jit(solution)/shard_map/nst,nsd->ntd/dot_general | solution.py:529
  96.9 0.0 copy-start
  96.9 2.7 %copy-done = bf16[16,64,2880]{2,1,0:T(8,128)(2,1)S(1)} copy-done((bf16[16,64,2880]{2,1,0:T(8,128)(2,1)S(1)}, bf16[16,64,2880]{2,1,0:T(8,128)(2,1)}, u32[]{:S(2)}) %copy-start) | copy-done | bytes 5898264
  99.7 32.7 %fold.1 = f32[64,1440]{1,0:T(8,128)S(1)} custom-call(bf16[16,64,2880]{2,1,0:T(8,128)(2,1)S(1)} %copy-done), custom_call_target="tpu_custom_call" | custom-call | tf_op jit(solution)/shard_map/fold/pallas_call | solution.py:393
  132.3 0.8 add_convert_fusion
  (8 shorter events, 0.1 us)
Async XLA Ops:
  3.9 0.8 copy-start.3
  4.8 0.8 copy-start.4
  5.6 0.7 copy-start.5
  18.1 4.4 %copy-start.6 = (bf16[2048,2880]{0,1:T(8,128)(2,1)S(1)}, bf16[2048,2880]{0,1:T(8,128)(2,1)}, u32[]{:S(2)}) copy-start(bf16[2048,2880]{0,1:T(8,128)(2,1)} %param.18) | copy-start | bytes 35389444
  22.4 3.7 %copy-start.2 = (bf16[64,2880]{1,0:T(8,128)(2,1)S(1)}, bf16[64,2880]{1,0:T(8,128)(2,1)}, u32[]{:S(2)}) copy-start(bf16[64,2880]{1,0:T(8,128)(2,1)} %refs_1_.3) | copy-start | bytes 1105924
  62.5 2.6 %copy-start.1 = (bf16[16,64,2880]{2,1,0:T(8,128)(2,1)}, bf16[16,64,2880]{2,1,0:T(8,128)(2,1)S(1)}, u32[]{:S(2)}) copy-start(bf16[16,64,2880]{2,1,0:T(8,128)(2,1)S(1)} %get-tuple-element.16) | copy-start | bytes 17694724
  96.9 2.7 %copy-start = (bf16[16,64,2880]{2,1,0:T(8,128)(2,1)S(1)}, bf16[16,64,2880]{2,1,0:T(8,128)(2,1)}, u32[]{:S(2)}) copy-start(bf16[16,64,2880]{2,1,0:T(8,128)(2,1)} %convolution_convert_fusion.refs_0_) | copy-start | bytes 17694724
